TPU v7x, 32 devices: a whole 2x2x4 slice. The times are simulated.
32 devices in a mesh: dp: 8 (over y, x, core), seq: 4 (over z).
Axes of the slice: x: 2, y: 2, z: 4, core: 2. Of those that a mesh axis runs over, the one named last changes fastest.
Arguments:
- text_in: bfloat16 [16, 256, 768], P('dp', 'seq'), may hold values from -6 to 6
- image_in: bfloat16 [16, 160, 1024], P('dp', 'seq'), may hold values from -6 to 6
- text_seg: int32 [16, 256], P('dp'), may hold values from 0 to 4, as said below
- image_seg: int32 [16, 160], P('dp'), may hold values from 0 to 4, as said below
- text_co_in: bfloat16 [768, 3072], replicated, may hold values from -0.21875 to 0.21875
- image_co_in: bfloat16 [1024, 3072], replicated, may hold values from -0.1875 to 0.1875
- text_co_out: bfloat16 [1024, 768], replicated, may hold values from -1 to 1
- image_co_out: bfloat16 [1024, 1024], replicated, may hold values from -1 to 1
- text_up: bfloat16 [768, 3072], replicated, may hold values from -0.21875 to 0.21875
- text_down: bfloat16 [3072, 768], replicated, may hold values from -0.15625 to 0.15625
- image_up: bfloat16 [1024, 1024], replicated, may hold values from -0.1875 to 0.1875
- image_down: bfloat16 [1024, 1024], replicated, may hold values from -0.25 to 0.25
- text_qkv: bfloat16 [768, 2304], replicated, may hold values from -0.21875 to 0.21875
- text_proj: bfloat16 [768, 768], replicated, may hold values from -1.25 to 1.25
- image_qkv: bfloat16 [1024, 3072], replicated, may hold values from -0.1875 to 0.1875
- image_proj: bfloat16 [1024, 1024], replicated, may hold values from -1 to 1
- text_gains: float32 [3, 768], replicated, may hold values from 0.25 to 1.75
- image_gains: float32 [3, 1024], replicated, may hold values from 0.25 to 1.75
- text_upstream: bfloat16 [16, 256, 768], P('dp', 'seq'), may hold values from -6 to 6
- image_upstream: bfloat16 [16, 160, 1024], P('dp', 'seq'), may hold values from -6 to 6
Outputs:
- text_result: bfloat16 [16, 256, 768], P('dp', 'seq')
- image_result: bfloat16 [16, 160, 1024], P('dp', 'seq')
- text_in_grad: float32 [16, 256, 768], P('dp', 'seq')
- image_in_grad: float32 [16, 160, 1024], P('dp', 'seq')
- text_co_in_grad: float32 [768, 3072], P('dp')
- image_co_in_grad: float32 [1024, 3072], P('dp')
- text_co_out_grad: float32 [1024, 768], P('dp')
- image_co_out_grad: float32 [1024, 1024], P('dp')
- text_up_grad: float32 [768, 3072], P('dp')
- text_down_grad: float32 [3072, 768], P('dp')
- image_up_grad: float32 [1024, 1024], P('dp')
- image_down_grad: float32 [1024, 1024], P('dp')
- text_qkv_grad: float32 [768, 2304], P('dp')
- text_proj_grad: float32 [768, 768], P('dp')
- image_qkv_grad: float32 [1024, 3072], P('dp')
- image_proj_grad: float32 [1024, 1024], P('dp')
- text_gains_grad: float32 [3, 768], replicated
- image_gains_grad: float32 [3, 1024], replicated
Inputs may be any that keep to these rules, and one draw needn't show every extreme that they name: `text_seg`: in every row the text slots hold four captions in order (ids 0, 1, 2, 3), each non-empty, then padding (id 4), never empty. `image_seg`: in every row the image slots hold the regions of four images in order (ids 0, 1, 2, 3), each non-empty, then padding (id 4), never empty.
All inputs are finite; a program needn't handle non-finite values.
Results may differ from a plain program's by a relative error of at most 0.024.
Values may be sent and summed in bfloat16 or wider, within the bound.
No kernel may reach another device: no remote copies, remote signals or barrier semaphores. Data moves between devices by JAX's collectives and lax.ppermute only.
A program may use at most 256 MiB of HBM per device.

v0:
```python
import functools
import types

import jax
import jax.numpy as jnp
from jax import lax
from jax.experimental import pallas as pl
from jax.experimental.pallas import tpu as pltpu
from jax.sharding import PartitionSpec as P

HT = 12
HI = 8
HC = 8

NORM_EPS = 1e-05

F32 = jnp.float32
BF16 = jnp.bfloat16
LOG2E = 1.4426950408889634
MASKED = -1.0e9 * LOG2E
SQRT_2_PI = 0.7978845608028654
GELU_CUBE = 0.044715
LANES = 128
TILE = 256
WIDE = 1536
WHOLE = 3072
GAIN_ROWS = 32
MIB = 1024 * 1024


def dot_nt(a, b):
    return lax.dot_general(a, b, (((1,), (1,)), ((), ())), preferred_element_type=F32)


def dot_nn(a, b):
    return lax.dot_general(a, b, (((1,), (0,)), ((), ())), preferred_element_type=F32)


def dot_tn(a, b):
    return lax.dot_general(a, b, (((0,), (0,)), ((), ())), preferred_element_type=F32)


class Copies:
    def __init__(self, sems):
        self.sems, self.used, self.leaving = sems, 0, []

    def fetch(self, src, dst):
        copy = pltpu.make_async_copy(src, dst, self.sems.at[self.used])
        self.used += 1
        copy.start()
        return copy

    def flush(self, src, dst):
        self.leaving.append(self.fetch(src, dst))

    def finish(self):
        for copy in self.leaving:
            copy.wait()


def nbytes(shape, dtype):
    total = jnp.dtype(dtype).itemsize
    dims = list(shape)
    dims[-1] = -(-dims[-1] // 128) * 128
    if len(dims) > 1:
        dims[-2] = -(-dims[-2] // 16) * 16
    for d in dims:
        total *= d
    return total


def kernel_call(name, body, scal, ins, outs, scratch, copies=64, extra=8):
    names = list(ins) + list(outs) + list(scratch)

    def kernel(scal_ref, *refs):
        k = types.SimpleNamespace(**dict(zip(names, refs)))
        moves = Copies(refs[-1])
        body(scal_ref, k, moves)
        moves.finish()

    def place(where):
        return pl.BlockSpec(memory_space=pltpu.HBM if where == "h" else pltpu.VMEM)

    def shape_of(shape, dtype, where):
        return pltpu.HBM(tuple(shape), dtype) if where == "h" else jax.ShapeDtypeStruct(shape, dtype)

    args = [
        pltpu.with_memory_space_constraint(x, pltpu.HBM) if where == "h" else x for x, where in ins.values()
    ]
    total = sum(nbytes(s, d) for s, d in scratch.values()) + extra * MIB
    got = pl.pallas_call(
        kernel,
        in_specs=[pl.BlockSpec(memory_space=pltpu.SMEM)] + [place(w) for _, w in ins.values()],
        out_specs=[place(w) for _, _, w in outs.values()],
        out_shape=[shape_of(*o) for o in outs.values()],
        scratch_shapes=[pltpu.VMEM(tuple(s), d) for s, d in scratch.values()]
        + [pltpu.SemaphoreType.DMA((copies,))],
        compiler_params=pltpu.CompilerParams(vmem_limit_bytes=total),
        name=name,
    )(scal, *args)
    return types.SimpleNamespace(**dict(zip(outs, got)))


def loop(count, body, unroll=1):
    def step(i, carry):
        body(i)
        return carry

    lax.fori_loop(0, count, step, 0, unroll=unroll)


def at(i, size):
    return pl.ds(pl.multiple_of(i * size, size), size)


def row_chunks(rows, body):
    size = next(c for c in (128, 80, 64, 32, 16) if rows % c == 0)
    loop(rows // size, lambda i: body(at(i, size)))


def tile_of(width, limit):
    parts = -(-width // limit)
    while width % (parts * TILE):
        parts += 1
    return width // parts


def pick(i, values):
    out = values[0]
    for k in range(1, len(values)):
        out = jnp.where(i == k, values[k], out)
    return out


def lane_halves(width):
    if width == LANES:
        return [None]
    lane = lax.broadcasted_iota(jnp.int32, (1, LANES), 1)
    return [(lane // width) == i for i in range(LANES // width)]


def keep_lanes(x, sel):
    return x if sel is None else jnp.where(sel, x, jnp.zeros_like(x))


def cols(ref, rows, tile):
    return ref[rows, tile * LANES : (tile + 1) * LANES]


def store_bias(bias_ref, down_ref, along_ref):
    for r in range(bias_ref.shape[0]):
        row = down_ref[r : r + 1].astype(F32)
        col = jnp.transpose(jnp.broadcast_to(row, (8, row.shape[1])))[:, :1]
        bias_ref[r] = jnp.where(col == along_ref[r : r + 1].astype(F32), 0.0, MASKED).astype(F32)


def attend(r, q_ref, kv_ref, bias, o_ref, p_ref, lq, lk, width):
    scale = width**-0.5 * LOG2E
    sels = lane_halves(width)
    n = o_ref.shape[1] // LANES
    qs, ks = at(r, lq), at(r, lk)
    for t in range(n):
        q, k, v = cols(q_ref, qs, t), cols(kv_ref, ks, n + t), cols(kv_ref, ks, 2 * n + t)
        out = None
        for i, sel in enumerate(sels):
            s = dot_nt(k, keep_lanes(q, sel)) * scale + bias
            e = jnp.exp2(s - jnp.max(s, axis=0, keepdims=True))
            p = (e * (1.0 / jnp.sum(e, axis=0, keepdims=True))).astype(BF16)
            p_ref[r, t * len(sels) + i] = p
            o = dot_tn(p, v)
            out = o if out is None else jnp.where(sel, o, out)
        o_ref[qs, t * LANES : (t + 1) * LANES] = out.astype(BF16)


def attend_wide(r, q_ref, kv_ref, bias, o_ref, p_ref, lq, lk):
    scale = LANES**-0.5 * LOG2E
    n = o_ref.shape[1] // LANES
    qs, ks = at(r, lq), at(r, lk)
    for t in range(n):
        q, k, v = cols(q_ref, qs, t), cols(kv_ref, ks, n + t), cols(kv_ref, ks, 2 * n + t)
        s = dot_nt(q, k) * scale + bias
        e = jnp.exp2(s - jnp.max(s, axis=1, keepdims=True))
        p = (e * (1.0 / jnp.sum(e, axis=1, keepdims=True))).astype(BF16)
        p_ref[r, t] = p
        o_ref[qs, t * LANES : (t + 1) * LANES] = dot_nn(p, v).astype(BF16)


def attend_wide_back(r, q_ref, kv_ref, da_ref, p_ref, dq_ref, dkv_ref, lq, lk):
    scale = LANES**-0.5
    n = da_ref.shape[1] // LANES
    qs, ks = at(r, lq), at(r, lk)
    for t in range(n):
        q, k, v = cols(q_ref, qs, t), cols(kv_ref, ks, n + t), cols(kv_ref, ks, 2 * n + t)
        da = cols(da_ref, qs, t)
        p = p_ref[r, t]
        pf = p.astype(F32)
        w = pf * dot_nt(da, v)
        ds = (w - pf * jnp.sum(w, axis=1, keepdims=True)).astype(BF16)
        dq_ref[qs, t * LANES : (t + 1) * LANES] = (dot_nn(ds, k) * scale).astype(BF16)
        dkv_ref[ks, (n + t) * LANES : (n + t + 1) * LANES] = (dot_tn(ds, q) * scale).astype(BF16)
        dkv_ref[ks, (2 * n + t) * LANES : (2 * n + t + 1) * LANES] = dot_tn(p, da).astype(BF16)


def attend_back(r, q_ref, kv_ref, da_ref, p_ref, dq_ref, dkv_ref, lq, lk, width):
    scale = width**-0.5
    sels = lane_halves(width)
    n = da_ref.shape[1] // LANES
    qs, ks = at(r, lq), at(r, lk)
    for t in range(n):
        q, k, v = cols(q_ref, qs, t), cols(kv_ref, ks, n + t), cols(kv_ref, ks, 2 * n + t)
        da = cols(da_ref, qs, t)
        dq = dk = dv = None
        for i, sel in enumerate(sels):
            p = p_ref[r, t * len(sels) + i]
            da_h = keep_lanes(da, sel)
            pf = p.astype(F32)
            w = pf * dot_nt(v, da_h)
            ds = (w - pf * jnp.sum(w, axis=0, keepdims=True)).astype(BF16)
            dv_h = dot_nn(p, da_h)
            dk_h = dot_nn(ds, keep_lanes(q, sel))
            dq_h = dot_tn(ds, keep_lanes(k, sel))
            dq = dq_h if dq is None else dq + dq_h
            dk = dk_h if dk is None else dk + dk_h
            dv = dv_h if dv is None else dv + dv_h
        dq_ref[qs, t * LANES : (t + 1) * LANES] = (dq * scale).astype(BF16)
        dkv_ref[ks, (n + t) * LANES : (n + t + 1) * LANES] = (dk * scale).astype(BF16)
        dkv_ref[ks, (2 * n + t) * LANES : (2 * n + t + 1) * LANES] = dv.astype(BF16)


def normalize(z):
    center = z - jnp.mean(z, axis=-1, keepdims=True)
    inv = lax.rsqrt(jnp.mean(center * center, axis=-1, keepdims=True) + NORM_EPS)
    return center * inv, inv


def fold_rows(x):
    return jnp.sum(x.reshape(x.shape[0] // 8, 8, x.shape[1]), axis=0)


def matmul_tiles(x_ref, w_ref, o_ref):
    n = o_ref.shape[1]
    tile = tile_of(n, WHOLE)

    def step(i):
        o_ref[:, at(i, tile)] = dot_nn(x_ref[...], w_ref[:, at(i, tile)]).astype(o_ref.dtype)

    loop(n // tile, step)


def norm_rows(acc_ref, res, gain, n_ref, inv_ref, low_ref=None):
    def chunk(rows):
        n, inv = normalize(acc_ref[rows] + res(rows))
        n_ref[rows] = n
        inv_ref[rows] = jnp.broadcast_to(inv, (inv.shape[0], LANES))
        if low_ref is not None:
            low_ref[rows] = (n * gain).astype(BF16)

    row_chunks(acc_ref.shape[0], chunk)


def norm_back_rows(dy_of, n_ref, inv_ref, gain, d_ref, low_ref, dg_ref):
    dg_ref[...] = jnp.zeros_like(dg_ref)

    def chunk(rows):
        dy = dy_of(rows)
        n = n_ref[rows]
        dn = dy * gain
        m1 = jnp.mean(dn, axis=-1, keepdims=True)
        m2 = jnp.mean(dn * n, axis=-1, keepdims=True)
        d = inv_ref[rows][:, :1] * (dn - m1 - n * m2)
        d_ref[rows] = d
        low_ref[rows] = d.astype(BF16)
        dg_ref[...] += fold_rows(dy * n)

    row_chunks(n_ref.shape[0], chunk)


def gelu_pair(v):
    v2 = v * v
    s = 0.5 + 0.5 * jnp.tanh(v * (SQRT_2_PI + (SQRT_2_PI * GELU_CUBE) * v2))
    a = v * s
    return a, s + a * (1.0 - s) * (2.0 * SQRT_2_PI + (6.0 * SQRT_2_PI * GELU_CUBE) * v2)


def ffn_tiles(x_ref, up_ref, down_ref, a_ref, slope_ref, acc_ref):
    width = tile_of(a_ref.shape[1], WIDE)

    def step(i):
        tile = at(i, width)
        a, slope = gelu_pair(dot_nn(x_ref[...], up_ref[:, tile]))
        a = a.astype(BF16)
        a_ref[:, tile] = a
        slope_ref[:, tile] = slope.astype(BF16)
        acc_ref[...] += dot_nn(a, down_ref[tile])

    acc_ref[...] = jnp.zeros_like(acc_ref)
    loop(a_ref.shape[1] // width, step)


def ffn_back_product(low_ref, down_ref, slope_ref, up_ref, dh_ref, acc_ref, ready):
    ready(low_ref, down_ref)
    dh = dot_nt(low_ref[...], down_ref[...])
    ready(slope_ref)
    dh = (dh * slope_ref[...].astype(F32)).astype(BF16)
    dh_ref[...] = dh
    ready(up_ref, acc_ref)
    acc_ref[...] += dot_nt(dh, up_ref[...])


def send_packed(cp, keep, send, far_keep, far_send, first, last):
    for near, far in ((send, far_send), (keep, far_keep)):
        cp.flush(near.at[:, first:last], far.at[:, first:last])


def wgrad_group(scal, cp, xs, ys, plan, ndp, keep, send, far_keep, far_send):
    by_member = all(off % 16 == 0 and (tiles * rows) % 16 == 0 for tiles, _, _, off, rows in plan)
    for x, y, p in zip(xs, ys, plan):
        wgrad_member(scal, x, y, keep, send, p, ndp)
        if by_member:
            send_packed(cp, keep, send, far_keep, far_send, p[3], p[3] + p[0] * p[4])
    if not by_member:
        send_packed(cp, keep, send, far_keep, far_send, 0, keep.shape[1])


def wgrad_member(scal_ref, x_ref, y_ref, keep_ref, send_ref, plan, ndp):
    tiles, total, split, off, rows = plan
    odd = scal_ref[0] == 1
    xt = jnp.transpose(x_ref[...])
    first = jnp.minimum(scal_ref[1] * tiles, total - tiles) if split else 0
    for t in range(tiles):
        g = dot_nn(xt, y_ref[:, at(first + t, TILE)]).astype(BF16)
        base = off + t * rows
        for j in range(ndp // 2):
            even_rows = g[2 * j * rows : (2 * j + 1) * rows]
            odd_rows = g[(2 * j + 1) * rows : (2 * j + 2) * rows]
            keep_ref[j, base : base + rows] = jnp.where(odd, odd_rows, even_rows)
            send_ref[j, base : base + rows] = jnp.where(odd, even_rows, odd_rows)


def pack_gains(gain_refs, rows_ref, keep_ref, send_ref, base):
    row = 0
    for ref in gain_refs:
        total = jnp.sum(ref[...], axis=0, keepdims=True)
        for c in range(0, ref.shape[1], TILE):
            rows_ref[row : row + 1] = total[:, c : c + TILE]
            row += 1
    for row in range(row, GAIN_ROWS):
        rows_ref[row : row + 1] = jnp.zeros((1, TILE), F32)
    low = rows_ref[...].astype(BF16)
    for j in range(keep_ref.shape[0]):
        keep_ref[j, base : base + GAIN_ROWS] = low
        send_ref[j, base : base + GAIN_ROWS] = low


def co_stage_body(scal, k, cp, *, rows, parts, count_t, count_i):
    pieces = [cp.fetch(getattr(k, f"part{i}"), k.staged.at[i]) for i in range(parts)]
    wa = cp.fetch(k.co_t, k.wa)
    wb = cp.fetch(k.co_i, k.wb)
    wo = cp.fetch(k.out_t, k.wo)
    wd = cp.fetch(k.down_t, k.wd)
    lt, li = parts * count_t, parts * count_i
    store_bias(k.bias, k.iseg, k.tseg)
    for piece in pieces:
        piece.wait()
    base = join_tiles(scal[1], k.staged, k.tx, count_t, rows, 0)
    wa.wait()
    matmul_tiles(k.tx, k.wa, k.tqkv)
    up_t = cp.fetch(k.up_t, k.wa)
    cp.flush(k.tx, k.o_tx)
    cp.flush(k.tqkv, k.o_tqkv)
    join_tiles(scal[1], k.staged, k.ix, count_i, rows, base)
    wb.wait()
    matmul_tiles(k.ix, k.wb, k.iqkv)
    wi = k.ix.shape[1]
    up_i = cp.fetch(k.up_i, k.wb.at[:, 0:wi])
    down_i = cp.fetch(k.down_i, k.wb.at[:, wi : 2 * wi])
    out_i = cp.fetch(k.out_i, k.wb.at[:, 2 * wi : 3 * wi])
    cp.flush(k.ix, k.o_ix)
    cp.flush(k.iqkv, k.o_iqkv)
    assert k.tatt.shape[1] == HC * LANES

    def heads(r):
        attend(r, k.tqkv, k.iqkv, k.bias[r], k.tatt, k.pt, lt, li, LANES)
        attend_wide(r, k.iqkv, k.tqkv, k.bias[r], k.iatt, k.pi, li, lt)

    loop(rows, heads)
    cp.flush(k.tatt, k.o_tatt)
    cp.flush(k.iatt, k.o_iatt)
    cp.flush(k.pt, k.o_pt)
    cp.flush(k.pi, k.o_pi)
    out_i.wait()
    matmul_tiles(k.iatt, k.wb.at[:, 2 * wi : 3 * wi], k.acc_i)
    ig = k.ig[...]
    norm_rows(k.acc_i, lambda r: k.ix[r].astype(F32), ig[0:1], k.in1, k.ir1, k.i1)
    up_i.wait()
    down_i.wait()
    ffn_tiles(k.i1, k.wb.at[:, 0:wi], k.wb.at[:, wi : 2 * wi], k.ia, k.isl, k.acc_i)
    norm_rows(k.acc_i, lambda r: k.in1[r] * ig[0:1], ig[1:2], k.in2, k.ir2, k.i2)
    for name in ("in1", "ir1", "i1", "ia", "isl", "in2", "ir2", "i2"):
        cp.flush(getattr(k, name), getattr(k, "o_" + name))
    wo.wait()
    matmul_tiles(k.tatt, k.wo, k.acc_t)
    tg = k.tg[...]
    norm_rows(k.acc_t, lambda r: k.tx[r].astype(F32), tg[0:1], k.tn1, k.tr1, k.t1)
    up_t.wait()
    wd.wait()
    for name in ("tn1", "tr1", "t1"):
        cp.flush(getattr(k, name), getattr(k, "o_" + name))
    ffn_tiles(k.t1, k.wa, k.wd, k.ta, k.tsl, k.acc_t)
    cp.flush(k.ta, k.o_ta)
    cp.flush(k.tsl, k.o_tsl)
    norm_rows(k.acc_t, lambda r: k.tn1[r] * tg[0:1], tg[1:2], k.tn2, k.tr2, k.t2)
    for name in ("t2", "tn2", "tr2"):
        cp.flush(getattr(k, name), getattr(k, "o_" + name))


def self_stage_body(scal, k, cp, *, rows, count_t, count_i):
    t2 = cp.fetch(k.h_t2, k.t2)
    wa = cp.fetch(k.qkv_t, k.wa)
    i2 = cp.fetch(k.h_i2, k.i2)
    wb = cp.fetch(k.qkv_i, k.wb)
    pa = cp.fetch(k.proj_t, k.pa)
    pb = cp.fetch(k.proj_i, k.pb)
    tn2 = cp.fetch(k.h_tn2, k.tn2)
    in2 = cp.fetch(k.h_in2, k.in2)
    store_bias(k.tbias, k.tseg, k.tseg)
    store_bias(k.ibias, k.iseg, k.iseg)
    lt = k.t2.shape[0] // rows
    li = k.i2.shape[0] // rows
    t2.wait()
    wa.wait()
    matmul_tiles(k.t2, k.wa, k.sqkv)
    cp.flush(k.sqkv, k.o_sqkv)
    i2.wait()
    wb.wait()
    matmul_tiles(k.i2, k.wb, k.uqkv)
    cp.flush(k.uqkv, k.o_uqkv)
    wt = k.tmix.shape[1] // HT
    wi = k.imix.shape[1] // HI

    def heads(r):
        attend(r, k.sqkv, k.sqkv, k.tbias[r], k.tmix, k.spt, lt, lt, wt)
        attend(r, k.uqkv, k.uqkv, k.ibias[r], k.imix, k.spi, li, li, wi)

    loop(rows, heads)
    for name in ("tmix", "imix", "spt", "spi"):
        cp.flush(getattr(k, name), getattr(k, "o_" + name))
    tn2.wait()
    in2.wait()
    z = scal[1]
    for mix, w, ready, acc, n2, g, n3, r3, res, count in (
        (k.tmix, k.pa, pa, k.acc_t, k.tn2, k.tg, k.tn3, k.tr3, k.tres, count_t),
        (k.imix, k.pb, pb, k.acc_i, k.in2, k.ig, k.in3, k.ir3, k.ires, count_i),
    ):
        ready.wait()
        matmul_tiles(mix, w, acc)
        gain = g[...]
        norm_rows(acc, lambda r, n2=n2, gain=gain: n2[r] * gain[1:2], None, n3, r3)
        length = mix.shape[0] // rows
        for r in range(rows):
            own = n3[pl.ds(pl.multiple_of(r * length + z * count, 8), count)]
            res[r] = (own * gain[2:3]).astype(BF16)
        for name in ("tn3", "tr3", "tres") if mix is k.tmix else ("in3", "ir3", "ires"):
            cp.flush(getattr(k, name), getattr(k, "o_" + name))


def self_back_body(scal, k, cp, *, rows, count_t, count_i, plan, ndp):
    ups = [cp.fetch(getattr(k, f"h_up{i}"), k.up.at[i]) for i in range(k.up.shape[0])]
    names = ("tn3", "tr3", "proj_t", "in3", "ir3", "proj_i", "sqkv", "spt", "uqkv", "spi")
    names += ("tmix", "t2", "i2")
    moves = {n: cp.fetch(getattr(k, "h_" + n), getattr(k, n)) for n in names}

    def ready(*which):
        for n in which:
            moves[n].wait()

    for copy in ups:
        copy.wait()
    base = join_tiles(scal[1], k.up, k.tup, count_t, rows, 0)
    join_tiles(scal[1], k.up, k.iup, count_i, rows, base)
    ready("tn3", "tr3", "proj_t")
    norm_back_rows(
        lambda r: k.tup[r].astype(F32), k.tn3, k.tr3, k.tg[2:3], k.o_d3, k.d3b, k.tdg
    )
    k.dmt[...] = dot_nt(k.d3b[...], k.proj_t[...]).astype(BF16)
    ready("in3", "ir3", "proj_i")
    norm_back_rows(
        lambda r: k.iup[r].astype(F32), k.in3, k.ir3, k.ig[2:3], k.o_e3, k.e3b, k.idg
    )
    k.dmi[...] = dot_nt(k.e3b[...], k.proj_i[...]).astype(BF16)
    ready("sqkv", "spt", "uqkv", "spi")
    lt, li = k.tup.shape[0] // rows, k.iup.shape[0] // rows
    wt = k.dmt.shape[1] // HT
    wi = k.dmi.shape[1] // HI

    def heads(r):
        attend_back(r, k.sqkv, k.sqkv, k.dmt, k.spt, k.o_dsqkv, k.o_dsqkv, lt, lt, wt)
        attend_back(r, k.uqkv, k.uqkv, k.dmi, k.spi, k.o_duqkv, k.o_duqkv, li, li, wi)

    loop(rows, heads)
    ready("tmix", "t2", "i2")
    xs, ys = (k.tmix, k.t2, k.i2), (k.d3b, k.o_dsqkv, k.o_duqkv)
    cp.flush(k.e3b, k.o_e3b)
    wgrad_group(scal, cp, xs, ys, plan, ndp, k.keep, k.send, k.o_keep, k.o_send)
    for name in ("tdg", "idg"):
        cp.flush(getattr(k, name), getattr(k, "o_" + name))


def chunked(cp, src, dst, axis, count=3):
    size = src.shape[axis] // count
    out = []
    for i in range(count):
        part = slice(i * size, (i + 1) * size)
        part = (slice(None), part) if axis == 1 else (part, slice(None))
        out.append((cp.fetch(src.at[part], dst.at[part]), part))
    return out


def qkv_back_body(scal, k, cp):
    wa = chunked(cp, k.qkv_t, k.wa, 0, 2)
    extra_t = [cp.fetch(k.h_tn2, k.tn2), cp.fetch(k.h_tr2, k.tr2)]
    wb = chunked(cp, k.qkv_i, k.wb, 0, 2)
    extra_i = [cp.fetch(k.h_in2, k.in2), cp.fetch(k.h_ir2, k.ir2)]
    for dx, w, ready, extra, acc, d3, n, inv, g, outs in (
        (k.dsqkv, k.wa, wa, extra_t, k.acc_t, k.d3, k.tn2, k.tr2, k.tg, ("d2", "d2b", "tdg")),
        (k.duqkv, k.wb, wb, extra_i, k.acc_i, k.e3, k.in2, k.ir2, k.ig, ("e2", "e2b", "idg")),
    ):
        for copy, (part, _) in ready:
            copy.wait()
            acc[:, part] = dot_nt(dx[...], w[part])
        for copy in extra:
            copy.wait()
        d2, low, dg = (getattr(k, name) for name in outs)
        norm_back_rows(lambda r, acc=acc, d3=d3: d3[r] + acc[r], n, inv, g[1:2], d2, low, dg)
        for name in outs:
            cp.flush(getattr(k, name), getattr(k, "o_" + name))


def ffn_back_body(scal, k, cp, *, plan, ndp):
    moves = {}

    def start(*names):
        for name in names:
            near = getattr(k, {"e2": "y1", "d2": "x1"}.get(name, name))
            moves[id(near)] = cp.fetch(getattr(k, "h_" + name), near)

    def ready(*refs):
        for ref in refs:
            moves.pop(id(ref)).wait()

    start("e2b", "down_i", "isl", "up_i", "e2", "d2b", "down_t", "tsl", "up_t", "d2")
    start("ta", "ia", "t1", "i1", "imix", "e3b")
    ffn_back_product(k.e2b, k.down_i, k.isl, k.up_i, k.dhi, k.y1, ready)
    cp.flush(k.y1, k.o_y1)
    ffn_back_product(k.d2b, k.down_t, k.tsl, k.up_t, k.dht, k.x1, ready)
    cp.flush(k.x1, k.o_x1)
    ready(k.ta, k.ia, k.t1, k.i1, k.imix, k.e3b)
    xs, ys = (k.ta, k.ia, k.t1, k.i1, k.imix), (k.d2b, k.e2b, k.dht, k.dhi, k.e3b)
    wgrad_group(scal, cp, xs, ys, plan, ndp, k.keep, k.send, k.o_keep, k.o_send)


def first_norm_back_body(scal, k, cp, *, rows, count_t, count_i):
    moves_t = [cp.fetch(getattr(k, "h_" + n), getattr(k, n)) for n in ("x1", "tn1", "tr1", "out_t")]
    moves_i = [cp.fetch(getattr(k, "h_" + n), getattr(k, n)) for n in ("y1", "in1", "ir1", "out_i")]
    *moves_t, out_t = moves_t
    *moves_i, out_i = moves_i
    z = scal[1]
    for moves, last, x1, n, inv, g, d1, low, dg, w, da, own, count in (
        (moves_t, out_t, k.x1, k.tn1, k.tr1, k.tg, k.d1, k.d1b, k.tdg, k.out_t, k.dat, k.own_t, count_t),
        (moves_i, out_i, k.y1, k.in1, k.ir1, k.ig, k.e1, k.e1b, k.idg, k.out_i, k.dai, k.own_i, count_i),
    ):
        for copy in moves:
            copy.wait()
        norm_back_rows(lambda r, x1=x1: x1[r], n, inv, g[0:1], d1, low, dg)
        last.wait()
        da[...] = dot_nt(low[...], w[...]).astype(BF16)
        length = x1.shape[0] // rows
        for r in range(rows):
            own[r] = d1[pl.ds(pl.multiple_of(r * length + z * count, 8), count)]
        text = x1 is k.x1
        for name in ("dat", "d1b", "own_t", "tdg") if text else ("dai", "e1b", "own_i", "idg"):
            cp.flush(getattr(k, name), getattr(k, "o_" + name))


def co_back_body(scal, k, cp, *, rows, parts, count_t, count_i, plan, last_plan, ndp, gains_at):
    names = ("tqkv", "pt", "dat", "iqkv", "pi", "dai", "iatt", "e1b", "tatt", "d1b", "ix", "tx")
    names += ("tdg1", "tdg2", "tdg3", "idg1", "idg2", "idg3")
    lt, li = parts * count_t, parts * count_i
    first = cp.used
    cp.used += 6 * rows

    def row_copies(r):
        out = []
        for i, name in enumerate(names[:6]):
            far, near = getattr(k, "h_" + name), getattr(k, name)
            part = r if name in ("pt", "pi") else at(r, near.shape[0] // rows)
            out.append(pltpu.make_async_copy(far.at[part], near.at[part], cp.sems.at[first + 6 * r + i]))
        return out

    for r in range(rows):
        for copy in row_copies(r):
            copy.start()
    moves = [cp.fetch(getattr(k, "h_" + n), getattr(k, n)) for n in names[6:]]

    def heads(r):
        for copy in row_copies(r):
            copy.wait()
        attend_back(r, k.tqkv, k.iqkv, k.dat, k.pt, k.dt, k.di, lt, li, LANES)
        attend_wide_back(r, k.iqkv, k.tqkv, k.dai, k.pi, k.di, k.dt, li, lt)

    loop(rows, heads)
    for copy in moves:
        copy.wait()
    xs, ys = (k.iatt, k.ix, k.tatt), (k.e1b, k.di, k.d1b)
    wgrad_group(scal, cp, xs, ys, plan, ndp, k.keep, k.send, k.o_keep, k.o_send)
    gains = (k.tdg1, k.tdg2, k.tdg3, k.idg1, k.idg2, k.idg3)
    pack_gains(gains, k.gain_rows, k.keep_last, k.send_last, gains_at)
    wgrad_member(scal, k.tx, k.dt, k.keep_last, k.send_last, last_plan, ndp)
    cp.flush(k.send_last, k.o_send_last)
    cp.flush(k.keep_last, k.o_keep_last)
    z = scal[1]
    for full, own, count in ((k.dt, k.o_dt, count_t), (k.di, k.o_di, count_i)):
        for r in range(rows):
            values = [
                full[(r * parts + i) * count : (r * parts + i + 1) * count] for i in range(parts)
            ]
            own[r] = pick(z, values)


def in_back_body(scal, k, cp):
    own_t = cp.fetch(k.h_d1, k.d1)
    own_i = cp.fetch(k.h_e1, k.e1)
    wa = chunked(cp, k.co_t, k.wa, 1)
    wb = chunked(cp, k.co_i, k.wb, 1)
    for dx, w, chunks, d1, out, own in (
        (k.dt, k.wa, wa, k.d1, k.gt, own_t),
        (k.di, k.wb, wb, k.e1, k.gi, own_i),
    ):
        own.wait()
        r, count, m = dx.shape
        flat = dx[...].reshape(r * count, m)
        total = d1[...].reshape(r * count, d1.shape[2])
        for copy, part in chunks:
            copy.wait()
            total = total + dot_nt(flat[part], w[part])
        out[...] = total.reshape(out.shape)
        cp.flush(out, k.o_dt if out is k.gt else k.o_di)


def pack_body(scal, k, cp, *, count):
    names = [f"{stream}{i}" for i in range(count) for stream in "ti"]
    moves = {name: cp.fetch(getattr(k, "h_" + name), getattr(k, name)) for name in names}
    for i in range(count):
        packed = getattr(k, f"s{i}")
        base = 0
        for name in (f"t{i}", f"i{i}"):
            moves[name].wait()
            ref = getattr(k, name)
            for c in range(0, ref.shape[2], TILE):
                for r in range(ref.shape[0]):
                    part = ref[r, :, c : c + TILE]
                    packed[base : base + part.shape[0]] = part
                    base += part.shape[0]
        cp.flush(packed, getattr(k, f"o{i}"))


def join_tiles(z, staged, full, count, rows, base):
    parts = staged.shape[0]
    for c in range(0, full.shape[1], TILE):
        for r in range(rows):
            values = [staged[i, base : base + count] for i in range(parts)]
            for i in range(parts):
                to = (r * parts + i) * count
                full[to : to + count, c : c + TILE] = pick(z ^ i, values)
            base += count
    return base


def unpack_body(scal, k, cp, *, plan, nseq, gains_at, gain_shapes):
    z = scal[1]
    pieces = [cp.fetch(getattr(k, f"h{i}"), getattr(k, f"p{i}")) for i in range(nseq)]
    def own_rows(first, last):
        if not hasattr(k, "parts"):
            return k.own[first:last].astype(F32)
        return sum(k.parts[i, first:last].astype(F32) for i in range(k.parts.shape[0]))

    if hasattr(k, "own"):
        cp.fetch(k.h_own, k.own).wait()
    if gain_shapes:
        sums = own_rows(gains_at, gains_at + GAIN_ROWS)
        row = 0
        for i, (count, width) in enumerate(gain_shapes):
            out = getattr(k, f"o_gain{i}")
            for g in range(count):
                for c in range(0, width, TILE):
                    out[g : g + 1, c : c + TILE] = sums[row : row + 1]
                    row += 1
    for i, (tiles, total, split, off, rows) in enumerate(plan):
        if not split:
            buf = getattr(k, f"b{i}")
            for t in range(tiles):
                buf[:, t * TILE : (t + 1) * TILE] = own_rows(off + t * rows, off + (t + 1) * rows)
            cp.flush(buf, getattr(k, f"o{i}"))
    for piece in pieces:
        piece.wait()
    for i, (tiles, total, split, off, rows) in enumerate(plan):
        if split:
            buf = getattr(k, f"b{i}")
            for s in range(nseq):
                ref = getattr(k, f"p{s}")
                first = jnp.minimum((z ^ s) * tiles, total - tiles)
                for t in range(tiles):
                    buf[:, at(first + t, TILE)] = ref[off + t * rows : off + (t + 1) * rows].astype(F32)
            cp.flush(buf, getattr(k, f"o{i}"))


class Comm:
    def __init__(self):
        self.nseq = lax.axis_size("seq")
        self.ndp = lax.axis_size("dp")
        self.z = lax.axis_index("seq")
        self.d = lax.axis_index("dp")
        self.scal = jnp.stack([self.d % 2, self.z]).astype(jnp.int32)

    def pieces_at_once(self, x):
        n = self.nseq
        return [x] + [lax.ppermute(x, "seq", [(i, i ^ k) for i in range(n)]) for k in range(1, n)]

    def pieces(self, x):
        n = self.nseq
        got = [x]
        for k in range(1, n):
            step = k & -k
            got.append(lax.ppermute(got[k ^ step], "seq", [(i, i ^ step) for i in range(n)]))
        return got

    def pack(self, *pairs):
        ins, outs, scratch = {}, {}, {}
        for i, (text, image) in enumerate(pairs):
            total = sum(x.shape[0] * x.shape[1] * (x.shape[2] // TILE) for x in (text, image))
            ins.update({f"h_t{i}": (text, "h"), f"h_i{i}": (image, "h")})
            scratch.update({f"t{i}": (text.shape, BF16), f"i{i}": (image.shape, BF16)})
            outs[f"o{i}"] = ((total, TILE), BF16, "h")
            scratch[f"s{i}"] = ((total, TILE), BF16)
        got = kernel_call(
            "pack",
            functools.partial(pack_body, count=len(pairs)),
            self.scal,
            ins,
            outs,
            scratch,
            copies=3 * len(pairs),
            extra=2,
        )
        return [getattr(got, name) for name in outs]

    def plan_of(self, members):
        plan = {}
        off = 0
        for want in (True, False):
            for i, (din, dout, split) in enumerate(members):
                if split != want:
                    continue
                total = dout // TILE
                tiles = -(-total // self.nseq) if split else total
                rows = din // self.ndp
                plan[i] = (tiles, total, split, off, rows)
                off += tiles * rows
            if want:
                split_rows = off
        return Plan(self, [plan[i] for i in range(len(members))], split_rows, off)


class Plan:
    def __init__(self, comm, members, split_rows, rows, gain_shapes=()):
        self.comm, self.members, self.split_rows, self.rows = comm, members, split_rows, rows
        self.gain_shapes = gain_shapes
        self.gains_at = rows

    def with_gains(self, shapes):
        self.gain_shapes = shapes
        self.rows += GAIN_ROWS
        return self

    def half(self):
        return (self.comm.ndp // 2, self.rows, TILE)

    def swap(self, keep, send):
        self.keep = keep
        self.got = lax.ppermute(send, "dp", [(i, i ^ 1) for i in range(self.comm.ndp)])

    def add(self):
        self.pair = (self.keep.astype(F32) + self.got.astype(F32)).astype(BF16)

    def cross(self):
        groups = [list(range(b, self.comm.ndp, 2)) for b in range(2)]
        self.parts = lax.all_to_all(
            self.pair, "dp", split_axis=0, concat_axis=0, tiled=True, axis_index_groups=groups
        )

    def along(self):
        def total(part):
            return jnp.sum(part.astype(F32), axis=0).astype(BF16)

        self.everyone = []
        if self.split_rows:
            self.everyone = self.comm.pieces(total(self.parts[:, : self.split_rows]))
        self.own = None
        if self.split_rows and self.rows > self.split_rows:
            self.own = total(self.parts[:, self.split_rows :])

    def unpack(self):
        plan = [(p[0], p[1], p[2], p[3] if p[2] else p[3] - self.split_rows, p[4]) for p in self.members]
        ins = {f"h{i}": (x, "h") for i, x in enumerate(self.everyone)}
        if self.own is not None:
            ins["h_own"] = (self.own, "h")
        elif not self.split_rows:
            ins["parts"] = (self.parts, "v")
        outs = {f"o{i}": ((p[4], p[1] * TILE), F32, "h") for i, p in enumerate(plan)}
        outs.update({f"o_gain{i}": (s, F32, "v") for i, s in enumerate(self.gain_shapes)})
        scratch = {f"p{i}": (x.shape, BF16) for i, x in enumerate(self.everyone)}
        if self.own is not None:
            scratch["own"] = (self.own.shape, BF16)
        scratch.update({f"b{i}": ((p[4], p[1] * TILE), F32) for i, p in enumerate(plan)})
        got = kernel_call(
            "unpack",
            functools.partial(
                unpack_body,
                plan=plan,
                nseq=len(self.everyone),
                gains_at=self.gains_at - self.split_rows,
                gain_shapes=self.gain_shapes,
            ),
            self.comm.scal,
            ins,
            outs,
            scratch,
            copies=16,
        )
        return [getattr(got, name) for name in outs]


def tie(*xs):
    return lax.optimization_barrier(xs)


def per_device(
    text_in,
    image_in,
    text_seg,
    image_seg,
    text_co_in,
    image_co_in,
    text_co_out,
    image_co_out,
    text_up,
    text_down,
    image_up,
    image_down,
    text_qkv,
    text_proj,
    image_qkv,
    image_proj,
    text_gains,
    image_gains,
    text_upstream,
    image_upstream,
):
    comm = Comm()
    scal = comm.scal
    n = comm.nseq
    rows, nt, dt = text_in.shape
    ni, di = image_in.shape[1:]
    lt, li = n * nt, n * ni
    tt, ti = rows * lt, rows * li
    dc = text_co_out.shape[0]
    ft, fi = text_up.shape[1], image_up.shape[1]
    segs = {"tseg": (text_seg, "v"), "iseg": (image_seg, "v")}
    gains = {"tg": (text_gains, "v"), "ig": (image_gains, "v")}

    (inputs,) = comm.pack((text_in, image_in))
    inputs = comm.pieces(inputs)
    text_upstream, image_upstream, inputs[1] = tie(text_upstream, image_upstream, inputs[1])
    (upstream,) = comm.pack((text_upstream, image_upstream))
    upstream, *inputs = tie(upstream, *inputs)
    upstream = comm.pieces_at_once(upstream)

    def saved(**shapes):
        return (
            {"o_" + name: (shape, dtype, "h") for name, (shape, dtype) in shapes.items()},
            {name: (shape, dtype) for name, (shape, dtype) in shapes.items()},
        )

    outs, scratch = saved(
        tx=((tt, dt), BF16),
        ix=((ti, di), BF16),
        tqkv=((tt, 3 * dc), BF16),
        iqkv=((ti, 3 * dc), BF16),
        tatt=((tt, dc), BF16),
        iatt=((ti, dc), BF16),
        pt=((rows, HC, li, lt), BF16),
        pi=((rows, HC, li, lt), BF16),
        tn1=((tt, dt), F32),
        tr1=((tt, LANES), F32),
        t1=((tt, dt), BF16),
        in1=((ti, di), F32),
        ir1=((ti, LANES), F32),
        i1=((ti, di), BF16),
        ta=((tt, ft), BF16),
        tsl=((tt, ft), BF16),
        ia=((ti, fi), BF16),
        isl=((ti, fi), BF16),
        tr2=((tt, LANES), F32),
        ir2=((ti, LANES), F32),
        tn2=((tt, dt), F32),
        t2=((tt, dt), BF16),
        in2=((ti, di), F32),
        i2=((ti, di), BF16),
    )
    scratch.update(
        staged=((n,) + inputs[0].shape, BF16),
        bias=((rows, li, lt), F32),
        wa=((dt, 3 * dc), BF16),
        wb=((di, 3 * dc), BF16),
        wo=((dc, dt), BF16),
        wd=((ft, dt), BF16),
        acc_t=((tt, dt), F32),
        acc_i=((ti, di), F32),
    )
    ins = {f"part{i}": (x, "h") for i, x in enumerate(inputs)}
    ins.update(
        co_t=(text_co_in, "h"),
        co_i=(image_co_in, "h"),
        out_t=(text_co_out, "h"),
        out_i=(image_co_out, "h"),
        up_t=(text_up, "h"),
        down_t=(text_down, "h"),
        up_i=(image_up, "h"),
        down_i=(image_down, "h"),
        **segs,
        **gains,
    )
    f1 = kernel_call(
        "co_stage",
        functools.partial(co_stage_body, rows=rows, parts=n, count_t=nt, count_i=ni),
        scal,
        ins,
        outs,
        scratch,
    )

    outs, scratch = saved(
        sqkv=((tt, 3 * dt), BF16),
        uqkv=((ti, 3 * di), BF16),
        tmix=((tt, dt), BF16),
        imix=((ti, di), BF16),
        spt=((rows, HT, lt, lt), BF16),
        spi=((rows, HI, li, li), BF16),
        tn3=((tt, dt), F32),
        tr3=((tt, LANES), F32),
        in3=((ti, di), F32),
        ir3=((ti, LANES), F32),
        tres=((rows, nt, dt), BF16),
        ires=((rows, ni, di), BF16),
    )
    scratch.update(
        wa=(text_qkv.shape, BF16),
        wb=(image_qkv.shape, BF16),
        pa=(text_proj.shape, BF16),
        pb=(image_proj.shape, BF16),
        acc_t=((tt, dt), F32),
        acc_i=((ti, di), F32),
        t2=((tt, dt), BF16),
        i2=((ti, di), BF16),
        tn2=((tt, dt), F32),
        in2=((ti, di), F32),
        tbias=((rows, lt, lt), F32),
        ibias=((rows, li, li), F32),
    )
    f2 = kernel_call(
        "self_stage",
        functools.partial(self_stage_body, rows=rows, count_t=nt, count_i=ni),
        scal,
        dict(
            h_t2=(f1.o_t2, "h"),
            h_i2=(f1.o_i2, "h"),
            h_tn2=(f1.o_tn2, "h"),
            h_in2=(f1.o_in2, "h"),
            qkv_t=(text_qkv, "h"),
            qkv_i=(image_qkv, "h"),
            proj_t=(text_proj, "h"),
            proj_i=(image_proj, "h"),
            **segs,
            **gains,
        ),
        outs,
        scratch,
    )

    group_1 = comm.plan_of([(dt, dt, True), (dt, 3 * dt, True), (di, 3 * di, True)])
    group_2 = comm.plan_of([(ft, dt, True), (fi, di, True), (dt, ft, True), (di, fi, True), (di, di, True)])
    group_3 = comm.plan_of([(dc, di, True), (di, 3 * dc, True), (dc, dt, True)])
    group_4 = comm.plan_of([(dt, 3 * dc, False)]).with_gains([text_gains.shape, image_gains.shape])

    def sources(**arrays):
        return (
            {"h_" + name: (x, "h") for name, x in arrays.items()},
            {name: (x.shape, x.dtype) for name, x in arrays.items()},
        )

    def packed(group, tag=""):
        shape = group.half()
        return (
            {"o_keep" + tag: (shape, BF16, "h"), "o_send" + tag: (shape, BF16, "h")},
            {"keep" + tag: (shape, BF16), "send" + tag: (shape, BF16)},
        )

    ins, scratch = sources(
        tn3=f2.o_tn3,
        tr3=f2.o_tr3,
        proj_t=text_proj,
        in3=f2.o_in3,
        ir3=f2.o_ir3,
        proj_i=image_proj,
        sqkv=f2.o_sqkv,
        spt=f2.o_spt,
        uqkv=f2.o_uqkv,
        spi=f2.o_spi,
        tmix=f2.o_tmix,
        t2=f1.o_t2,
        i2=f1.o_i2,
    )
    ins.update({f"h_up{i}": (x, "h") for i, x in enumerate(upstream)})
    outs, more = packed(group_1)
    scratch.update(
        **more,
        up=((n,) + upstream[0].shape, BF16),
        tup=((tt, dt), BF16),
        iup=((ti, di), BF16),
        d3b=((tt, dt), BF16),
        e3b=((ti, di), BF16),
        dmt=((tt, dt), BF16),
        dmi=((ti, di), BF16),
        tdg=((8, dt), F32),
        idg=((8, di), F32),
    )
    outs.update(
        o_e3b=((ti, di), BF16, "h"),
        o_d3=((tt, dt), F32, "v"),
        o_e3=((ti, di), F32, "v"),
        o_dsqkv=((tt, 3 * dt), BF16, "v"),
        o_duqkv=((ti, 3 * di), BF16, "v"),
        o_tdg=((8, dt), F32, "h"),
        o_idg=((8, di), F32, "h"),
    )
    b1 = kernel_call(
        "self_back",
        functools.partial(
            self_back_body, rows=rows, count_t=nt, count_i=ni, plan=group_1.members, ndp=comm.ndp
        ),
        scal,
        {**ins, **gains},
        outs,
        scratch,
    )
    group_1.swap(b1.o_keep, b1.o_send)

    ins, scratch = sources(tn2=f1.o_tn2, tr2=f1.o_tr2, in2=f1.o_in2, ir2=f1.o_ir2)
    outs, more = saved(
        d2=((tt, dt), F32),
        e2=((ti, di), F32),
        d2b=((tt, dt), BF16),
        e2b=((ti, di), BF16),
        tdg=((8, dt), F32),
        idg=((8, di), F32),
    )
    scratch.update(
        **more,
        wa=(text_qkv.shape, BF16),
        wb=(image_qkv.shape, BF16),
        acc_t=((tt, dt), F32),
        acc_i=((ti, di), F32),
    )
    b2 = kernel_call(
        "qkv_back",
        qkv_back_body,
        scal,
        dict(
            **ins,
            qkv_t=(text_qkv, "h"),
            qkv_i=(image_qkv, "h"),
            dsqkv=(b1.o_dsqkv, "v"),
            duqkv=(b1.o_duqkv, "v"),
            d3=(b1.o_d3, "v"),
            e3=(b1.o_e3, "v"),
            **gains,
        ),
        outs,
        scratch,
    )
    group_1.got, d2, e2, d2b, e2b = tie(group_1.got, b2.o_d2, b2.o_e2, b2.o_d2b, b2.o_e2b)
    group_1.add()
    group_1.cross()

    ins, scratch = sources(
        down_i=image_down,
        isl=f1.o_isl,
        up_i=image_up,
        down_t=text_down,
        tsl=f1.o_tsl,
        up_t=text_up,
        ia=f1.o_ia,
        i1=f1.o_i1,
        ta=f1.o_ta,
        t1=f1.o_t1,
        d2b=d2b,
        e2b=e2b,
        imix=f2.o_imix,
        e3b=b1.o_e3b,
    )
    ins.update(h_d2=(d2, "h"), h_e2=(e2, "h"))
    outs, more = packed(group_2)
    scratch.update(x1=((tt, dt), F32), y1=((ti, di), F32))
    scratch.update(**more, dht=((tt, ft), BF16), dhi=((ti, fi), BF16))
    b3 = kernel_call(
        "ffn_back",
        functools.partial(ffn_back_body, plan=group_2.members, ndp=comm.ndp),
        scal,
        ins,
        dict(**outs, o_x1=((tt, dt), F32, "h"), o_y1=((ti, di), F32, "h")),
        scratch,
    )
    group_1.parts, x1, y1, keep, send = tie(
        group_1.parts, b3.o_x1, b3.o_y1, b3.o_keep, b3.o_send
    )
    group_2.swap(keep, send)
    group_1.along()

    ins, scratch = sources(
        x1=x1, y1=y1, tn1=f1.o_tn1, tr1=f1.o_tr1, out_t=text_co_out, in1=f1.o_in1, ir1=f1.o_ir1, out_i=image_co_out
    )
    outs, more = saved(
        d1b=((tt, dt), BF16),
        e1b=((ti, di), BF16),
        dat=((tt, dc), BF16),
        dai=((ti, dc), BF16),
        own_t=((rows, nt, dt), F32),
        own_i=((rows, ni, di), F32),
        tdg=((8, dt), F32),
        idg=((8, di), F32),
    )
    scratch.update(**more, d1=((tt, dt), F32), e1=((ti, di), F32))
    b4 = kernel_call(
        "first_norm_back",
        functools.partial(first_norm_back_body, rows=rows, count_t=nt, count_i=ni),
        scal,
        dict(**ins, **gains),
        outs,
        scratch,
    )
    group_2.got, dat, dai = tie(group_2.got, b4.o_dat, b4.o_dai)
    group_2.add()
    group_2.cross()

    ins, scratch = sources(
        tqkv=f1.o_tqkv,
        pt=f1.o_pt,
        iqkv=f1.o_iqkv,
        pi=f1.o_pi,
        tatt=f1.o_tatt,
        iatt=f1.o_iatt,
        tx=f1.o_tx,
        ix=f1.o_ix,
        dat=dat,
        dai=dai,
        d1b=b4.o_d1b,
        e1b=b4.o_e1b,
        tdg1=b4.o_tdg,
        tdg2=b2.o_tdg,
        tdg3=b1.o_tdg,
        idg1=b4.o_idg,
        idg2=b2.o_idg,
        idg3=b1.o_idg,
    )
    outs, more = packed(group_3)
    outs_last, more_last = packed(group_4, "_last")
    outs.update(outs_last)
    scratch.update(
        **more, **more_last, dt=((tt, 3 * dc), BF16), di=((ti, 3 * dc), BF16), gain_rows=((GAIN_ROWS, TILE), F32)
    )
    b5 = kernel_call(
        "co_back",
        functools.partial(
            co_back_body,
            rows=rows,
            parts=n,
            count_t=nt,
            count_i=ni,
            plan=group_3.members,
            last_plan=group_4.members[0],
            ndp=comm.ndp,
            gains_at=group_4.gains_at,
        ),
        scal,
        ins,
        dict(
            **outs,
            o_dt=((rows, nt, 3 * dc), BF16, "v"),
            o_di=((rows, ni, 3 * dc), BF16, "v"),
        ),
        scratch,
    )
    (
        group_1.everyone[1],
        group_1.everyone[2],
        group_2.parts,
        dt_own,
        di_own,
        keep,
        send,
        keep_last,
        send_last,
    ) = tie(
        group_1.everyone[1],
        group_1.everyone[2],
        group_2.parts,
        b5.o_dt,
        b5.o_di,
        b5.o_keep,
        b5.o_send,
        b5.o_keep_last,
        b5.o_send_last,
    )
    group_3.swap(keep, send)
    group_4.swap(keep_last, send_last)
    group_2.along()
    b6 = kernel_call(
        "in_back",
        in_back_body,
        scal,
        dict(
            co_t=(text_co_in, "h"),
            co_i=(image_co_in, "h"),
            dt=(dt_own, "v"),
            di=(di_own, "v"),
            h_d1=(b4.o_own_t, "h"),
            h_e1=(b4.o_own_i, "h"),
        ),
        dict(o_dt=((rows, nt, dt), F32, "h"), o_di=((rows, ni, di), F32, "h")),
        dict(
            gt=((rows, nt, dt), F32),
            gi=((rows, ni, di), F32),
            wa=(text_co_in.shape, BF16),
            wb=(image_co_in.shape, BF16),
            d1=((rows, nt, dt), F32),
            e1=((rows, ni, di), F32),
        ),
    )
    group_1.everyone[3], group_3.got, group_4.got, text_in_grad, image_in_grad = tie(
        group_1.everyone[3], group_3.got, group_4.got, b6.o_dt, b6.o_di
    )
    group_3.add()
    group_3.cross()
    group_4.add()
    group_2.everyone[1], group_2.everyone[2], group_3.parts, group_4.pair = tie(
        group_2.everyone[1], group_2.everyone[2], group_3.parts, group_4.pair
    )
    group_4.cross()
    group_3.along()
    text_proj_grad, text_qkv_grad, image_qkv_grad = group_1.unpack()
    (
        text_down_grad,
        image_down_grad,
        text_up_grad,
        image_up_grad,
        image_proj_grad,
    ) = group_2.unpack()
    group_4.along()
    text_co_in_grad, text_gains_grad, image_gains_grad = group_4.unpack()
    *group_3.everyone, text_co_in_grad, text_gains_grad, image_gains_grad = tie(
        *group_3.everyone, text_co_in_grad, text_gains_grad, image_gains_grad
    )
    image_co_out_grad, image_co_in_grad, text_co_out_grad = group_3.unpack()
    return (
        f2.o_tres,
        f2.o_ires,
        text_in_grad,
        image_in_grad,
        text_co_in_grad,
        image_co_in_grad,
        text_co_out_grad,
        image_co_out_grad,
        text_up_grad,
        text_down_grad,
        image_up_grad,
        image_down_grad,
        text_qkv_grad,
        text_proj_grad,
        image_qkv_grad,
        image_proj_grad,
        text_gains_grad,
        image_gains_grad,
    )


def solution(mesh):
    slots = P("dp", "seq", None)
    rows = P("dp", None)
    return jax.shard_map(
        per_device,
        mesh=mesh,
        in_specs=(slots, slots, rows, rows) + (P(),) * 14 + (slots, slots),
        out_specs=(slots,) * 4 + (rows,) * 12 + (P(), P()),
        check_vma=False,
    )
```

profile of v0, /device:TPU:0, one launch (start us, length us, event | category | flops | bytes accessed | tf_op | source)
XLA Modules:
  0.0 279.5 jit_solution(14658919982826985154)
XLA Ops:
  0.7 2.3 pack.2.refs_0_
  3.1 4.1 %collective-permute-start.1 = (bf16[704,256]{1,0:T(8,128)(2,1)}, bf16[704,256]{1,0:T(8,128)(2,1)S(1)}, u32[]{:S(2)}, u32[]{:S(2)}) collective-permute-start(bf16[704,256]{1,0:T(8,128)(2,1)} %pack.2.refs_0_), channel_id=1, source_target_pairs={{0,2},{1,3},{2,0},{3,1},{4,6},{5,7},{6,4},{7,5},{8,10},{9,11},{10,... | collective-permute-start | bytes 1081352 | tf_op jit(solution)/shard_map/ppermute | solution.py:734
  8.8 14.9 %collective-permute-done.1.refs_2_ = bf16[704,256]{1,0:T(8,128)(2,1)S(1)} collective-permute-done((bf16[704,256]{1,0:T(8,128)(2,1)}, bf16[704,256]{1,0:T(8,128)(2,1)S(1)}, u32[]{:S(2)}, u32[]{:S(2)}) %collective-permute-start.1) | collective-permute-done | bytes 360480 | tf_op jit(solution)/shard_map/ppermute | solution.py:734
  24.4 2.3 pack.3.refs_13_
  26.7 6.4 %collective-permute-done.2.refs_3_ = bf16[704,256]{1,0:T(8,128)(2,1)S(1)} collective-permute-done((bf16[704,256]{1,0:T(8,128)(2,1)S(1)}, bf16[704,256]{1,0:T(8,128)(2,1)S(1)}, u32[]{:S(2)}, u32[]{:S(2)}) %collective-permute-start.2) | collective-permute-done | bytes 360480 | tf_op jit(solution)/shard_map/ppermute | solution.py:734
  33.2 4.2 %collective-permute-start.5 = (bf16[704,256]{1,0:T(8,128)(2,1)}, bf16[704,256]{1,0:T(8,128)(2,1)S(1)}, u32[]{:S(2)}, u32[]{:S(2)}) collective-permute-start(bf16[704,256]{1,0:T(8,128)(2,1)} %pack.3.refs_13_), channel_id=1, source_target_pairs={{0,3},{1,2},{2,1},{3,0},{4,7},{5,6},{6,5},{7,4},{8,11},{9,10},{10,... | collective-permute-start | bytes 1081352 | tf_op jit(solution)/shard_map/ppermute | solution.py:727
  38.0 29.3 %co_stage.1 = (bf16[512,768]{1,0:T(8,128)(2,1)}, bf16[320,1024]{1,0:T(8,128)(2,1)}, bf16[512,3072]{1,0:T(8,128)(2,1)}, bf16[320,3072]{1,0:T(8,128)(2,1)}, bf16[5...) custom-call(s32[2]{0:T(128)} %copy-done.2, ...), custom_call_target="tpu_custom_call" | custom-call | tf_op jit(solution)/shard_map/co_stage/pallas_call | solution.py:91
  68.0 18.8 %self_stage.1 = (bf16[512,2304]{1,0:T(8,128)(2,1)}, bf16[320,3072]{1,0:T(8,128)(2,1)}, bf16[512,768]{1,0:T(8,128)(2,1)}, bf16[320,1024]{1,0:T(8,128)(2,1)}, bf16...) custom-call(s32[2]{0:T(128)S(1)} %copy-done.3, ...), custom_call_target="tpu_custom_call" | custom-call | tf_op jit(solution)/shard_map/self_stage/pallas_call | solution.py:91
  87.8 20.6 %self_back.1 = (bf16[4,768,256]{2,1,0:T(8,128)(2,1)}, bf16[4,768,256]{2,1,0:T(8,128)(2,1)}, bf16[320,1024]{1,0:T(8,128)(2,1)}, f32[512,768]{1,0:T(8,128)S(1)}, f...) custom-call(s32[2]{0:T(128)S(1)} %copy-done.3, ...), custom_call_target="tpu_custom_call" | custom-call | tf_op jit(solution)/shard_map/self_back/pallas_call | solution.py:91
  108.5 11.2 %qkv_back.1 = (f32[512,768]{1,0:T(8,128)}, f32[320,1024]{1,0:T(8,128)}, bf16[512,768]{1,0:T(8,128)(2,1)}, bf16[320,1024]{1,0:T(8,128)(2,1)}, f32[8,768]{1,0:T(8,128)}, /*index=5*/f32[8,1024]{1,0:T(8,128)}) custom-call(s32[2]{0:T(128)S(1)} %copy-done.3, f32[512,768]{1,0:T(8,128)} %get-tuple-element.158.refs_2_.refs_0_, ...), custom_call_target="tpu_custom_call" | custom-call | tf_op jit(solution)/shard_map/qkv_back/pallas_call | solution.py:91
  121.3 4.0 %all-to-all-start = ((bf16[4,768,256]{2,1,0:T(8,128)(2,1)}), bf16[4,768,256]{2,1,0:T(8,128)(2,1)S(1)}, u32[]{:S(2)}, u32[]{:S(2)}) async-start(bf16[4,768,256]{2,1,0:T(8,128)(2,1)} %add_convert_fusion.2), calls=%async_computation | async-start | bytes 3145728 | tf_op jit(solution)/shard_map/all_to_all | solution.py:797
  125.4 16.8 %ffn_back.1 = (bf16[4,1056,256]{2,1,0:T(8,128)(2,1)}, bf16[4,1056,256]{2,1,0:T(8,128)(2,1)}, f32[512,768]{1,0:T(8,128)}, f32[320,1024]{1,0:T(8,128)}) custom-call(s32[2]{0:T(128)S(1)} %copy-done.4, bf16[1024,1024]{1,0:T(8,128)(2,1)} %refs_0_.5, bf16[320,1024]{1,0:T(8,128)(2,1)} %get-tuple-element.185.refs_1_, bf16[1024,1024]{1,0:T(8,128)(2,1)} %refs_2_.3, ...), custom_call_target="tpu_custom_call" | custom-call | tf_op jit(solution)/shard_map/ffn_back/pallas_call | solution.py:91
  142.2 3.1 %all-to-all-done = bf16[4,768,256]{2,1,0:T(8,128)(2,1)S(1)} async-done(((bf16[4,768,256]{2,1,0:T(8,128)(2,1)}), bf16[4,768,256]{2,1,0:T(8,128)(2,1)S(1)}, u32[]{:S(2)}, u32[]{:S(2)}) %all-to-all-start) | async-done | bytes 1572896 | tf_op jit(solution)/shard_map/all_to_all | solution.py:797
  145.3 8.5 %first_norm_back.1 = (bf16[512,768]{1,0:T(8,128)(2,1)}, bf16[320,1024]{1,0:T(8,128)(2,1)}, bf16[512,1024]{1,0:T(8,128)(2,1)}, bf16[320,1024]{1,0:T(8,128)(2,1)},...) custom-call(s32[2]{0:T(128)S(1)} %copy-done.4, ...), custom_call_target="tpu_custom_call" | custom-call | tf_op jit(solution)/shard_map/first_norm_back/pallas_call | solution.py:91
  155.8 3.8 %all-to-all-start.1 = ((bf16[4,1056,256]{2,1,0:T(8,128)(2,1)}), bf16[4,1056,256]{2,1,0:T(8,128)(2,1)S(1)}, u32[]{:S(2)}, u32[]{:S(2)}) async-start(bf16[4,1056,256]{2,1,0:T(8,128)(2,1)} %add_convert_fusion.1), calls=%async_computation.1 | async-start | bytes 4325376 | tf_op jit(solution)/shard_map/all_to_all | solution.py:797
  159.7 2.5 reduce_sum.36.refs_0_
  163.6 2.9 %collective-permute-start.7 = (bf16[768,256]{1,0:T(8,128)(2,1)}, bf16[768,256]{1,0:T(8,128)(2,1)}, u32[]{:S(2)}, u32[]{:S(2)}) collective-permute-start(bf16[768,256]{1,0:T(8,128)(2,1)} %reduce_sum.36.refs_0_), channel_id=1, source_target_pairs={{0,2},{1,3},{2,0},{3,1},{4,6},{5,7},{6,4},{7,5},{8,10},{9,11},{10,... | collective-permute-start | bytes 1179656 | tf_op jit(solution)/shard_map/ppermute | solution.py:734
  166.5 19.8 %co_back.1 = (bf16[4,640,256]{2,1,0:T(8,128)(2,1)}, bf16[4,640,256]{2,1,0:T(8,128)(2,1)}, bf16[4,1184,256]{2,1,0:T(8,128)(2,1)}, bf16[4,1184,256]{2,1,0:T(8,128)...) custom-call(s32[2]{0:T(128)S(1)} %copy-done.4, bf16[512,3072]{1,0:T(8,128)(2,1)} %get-tuple-element.213.refs_0_, ...), custom_call_target="tpu_custom_call" | custom-call | tf_op jit(solution)/shard_map/co_back/pallas_call | solution.py:91
  187.6 8.7 %in_back.1 = (f32[2,64,768]{2,1,0:T(8,128)}, f32[2,40,1024]{2,1,0:T(8,128)}) custom-call(s32[2]{0:T(128)S(1)} %copy-done.4, bf16[768,3072]{1,0:T(8,128)(2,1)} %refs_0_.6, bf16[1024,3072]{1,0:T(8,128)(2,1)} %refs_1_.4, bf16[2,64,3072]{2,1,0:T(8,128)(2,1)S(1)} %get-tuple-element.239.refs_2_, bf16[2,40,3072]{2,1,0:T(8,128)(2,1)S(1)} %get-tuple-element.240.refs_3_, ...), custom_call_target="tpu_custom_call" | custom-call | tf_op jit(solution)/shard_map/in_back/pallas_call | solution.py:91
  196.3 2.6 collective-permute-done.8.refs_3_
  201.1 4.4 %all-to-all-start.2 = ((bf16[4,640,256]{2,1,0:T(8,128)(2,1)}), bf16[4,640,256]{2,1,0:T(8,128)(2,1)S(1)}, u32[]{:S(2)}, u32[]{:S(2)}) async-start(bf16[4,640,256]{2,1,0:T(8,128)(2,1)} %add_convert_fusion.3), calls=%async_computation.2 | async-start | bytes 2621440 | tf_op jit(solution)/shard_map/all_to_all | solution.py:797
  208.9 4.4 %add_convert_fusion = bf16[4,1184,256]{2,1,0:T(8,128)(2,1)} fusion(bf16[4,1184,256]{2,1,0:T(8,128)(2,1)} %collective-permute-done.12, bf16[4,1184,256]{2,1,0:T(8,128)(2,1)} %get-tuple-element.250), kind=kLoop, calls=%fused_computation | loop fusion | flops 4849664 | bytes 7274496 | tf_op jit(solution)/shard_map/convert_element_type | solution.py:793
  213.3 19.3 %collective-permute-done.14.refs_2_ = bf16[1056,256]{1,0:T(8,128)(2,1)S(1)} collective-permute-done((bf16[1056,256]{1,0:T(8,128)(2,1)}, bf16[1056,256]{1,0:T(8,128)(2,1)S(1)}, u32[]{:S(2)}, u32[]{:S(2)}) %collective-permute-start.14) | collective-permute-done | bytes 540704 | tf_op jit(solution)/shard_map/ppermute | solution.py:734
  234.4 3.9 %all-to-all-start.3 = ((bf16[4,1184,256]{2,1,0:T(8,128)(2,1)}), bf16[4,1184,256]{2,1,0:T(8,128)(2,1)S(1)}, u32[]{:S(2)}, u32[]{:S(2)}) async-start(bf16[4,1184,256]{2,1,0:T(8,128)(2,1)} %add_convert_fusion), calls=%async_computation.3 | async-start | bytes 4849664 | tf_op jit(solution)/shard_map/all_to_all | solution.py:797
  240.1 2.3 collective-permute-start.18
  242.4 14.2 %collective-permute-done.16.refs_2_ = bf16[640,256]{1,0:T(8,128)(2,1)S(1)} collective-permute-done((bf16[640,256]{1,0:T(8,128)(2,1)S(1)}, bf16[640,256]{1,0:T(8,128)(2,1)S(1)}, u32[]{:S(2)}, u32[]{:S(2)}) %collective-permute-start.16) | collective-permute-done | bytes 327712 | tf_op jit(solution)/shard_map/ppermute | solution.py:734
  256.6 3.7 %unpack.7 = (f32[96,768]{1,0:T(8,128)}, f32[96,2304]{1,0:T(8,128)}, f32[128,3072]{1,0:T(8,128)}) custom-call(s32[2]{0:T(128)S(1)} %copy-done.4, bf16[768,256]{1,0:T(8,128)(2,1)} %reduce_sum.36.refs_0_, bf16[768,256]{1,0:T(8,128)(2,1)} %copy-done.15, bf16[768,256]{1,0:T(8,128)(2,1)} %collective-permute-done.7.refs_2_, bf16[768,256]{1,0:T(8,128)(2,1)} %copy-done.16), custom_call_target="tpu_custom_call" | custom-call | tf_op jit(solution)/shard_map/unpack/pallas_call | solution.py:91
  260.3 2.4 collective-permute-done.18.refs_3_
  263.5 4.3 %unpack.6 = (f32[384,768]{1,0:T(8,128)}, f32[128,1024]{1,0:T(8,128)}, f32[96,3072]{1,0:T(8,128)}, f32[128,1024]{1,0:T(8,128)}, f32[128,1024]{1,0:T(8,128)}) custom-call(s32[2]{0:T(128)S(1)} %copy-done.4, bf16[1056,256]{1,0:T(8,128)(2,1)} %reduce_sum.37.refs_0_, bf16[1056,256]{1,0:T(8,128)(2,1)} %collective-permute-done.13.refs_1_, ...), custom_call_target="tpu_custom_call" | custom-call | tf_op jit(solution)/shard_map/unpack/pallas_call | solution.py:91
  267.8 2.6 unpack.4
  270.4 5.3 %collective-permute-done.17.refs_3_ = bf16[640,256]{1,0:T(8,128)(2,1)} collective-permute-done((bf16[640,256]{1,0:T(8,128)(2,1)S(1)}, bf16[640,256]{1,0:T(8,128)(2,1)}, u32[]{:S(2)}, u32[]{:S(2)}) %collective-permute-start.17) | collective-permute-done | bytes 327712 | tf_op jit(solution)/shard_map/ppermute | solution.py:734
  275.7 3.5 %unpack.5 = (f32[128,1024]{1,0:T(8,128)}, f32[128,3072]{1,0:T(8,128)}, f32[128,768]{1,0:T(8,128)}) custom-call(s32[2]{0:T(128)S(1)} %copy-done.4, bf16[640,256]{1,0:T(8,128)(2,1)} %copy-done.12, bf16[640,256]{1,0:T(8,128)(2,1)} %copy-done.24, bf16[640,256]{1,0:T(8,128)(2,1)} %copy-done.23, bf16[640,256]{1,0:T(8,128)(2,1)} %collective-permute-done.17.refs_3_), custom_call_target="tpu_custom_call" | custom-call | tf_op jit(solution)/shard_map/unpack/pallas_call | solution.py:91
  (86 shorter events, 20.9 us)
Async XLA Ops:
  0.7 37.2 %copy-start.2 = (s32[2]{0:T(128)}, s32[2]{0:T(128)S(1)}, u32[]{:S(2)}) copy-start(s32[2]{0:T(128)S(1)} %pad_add_fusion.scal_ref) | copy-start | bytes 28
  3.1 20.6 %collective-permute-start.1 = (bf16[704,256]{1,0:T(8,128)(2,1)}, bf16[704,256]{1,0:T(8,128)(2,1)S(1)}, u32[]{:S(2)}, u32[]{:S(2)}) collective-permute-start(bf16[704,256]{1,0:T(8,128)(2,1)} %pack.2.refs_0_), channel_id=1, source_target_pairs={{0,2},{1,3},{2,0},{3,1},{4,6},{5,7},{6,4},{7,5},{8,10},{9,11},{10,... | collective-permute-start | bytes 1081352 | tf_op jit(solution)/shard_map/ppermute | solution.py:734
  7.2 17.2 %collective-permute-start = (bf16[704,256]{1,0:T(8,128)(2,1)}, bf16[704,256]{1,0:T(8,128)(2,1)S(1)}, u32[]{:S(2)}, u32[]{:S(2)}) collective-permute-start(bf16[704,256]{1,0:T(8,128)(2,1)} %pack.2.refs_0_), channel_id=1, source_target_pairs={{0,1},{1,0},{2,3},{3,2},{4,5},{5,4},{6,7},{7,6},{8,9},{9,8},{10,11... | collective-permute-start | bytes 1081352 | tf_op jit(solution)/shard_map/ppermute | solution.py:734
  23.6 14.3 %copy-start.17 = (bf16[704,256]{1,0:T(8,128)(2,1)}, bf16[704,256]{1,0:T(8,128)(2,1)S(1)}, u32[]{:S(2)}) copy-start(bf16[704,256]{1,0:T(8,128)(2,1)S(1)} %collective-permute-done.1.refs_2_) | copy-start | bytes 1081348
  23.6 9.5 %collective-permute-start.2 = (bf16[704,256]{1,0:T(8,128)(2,1)S(1)}, bf16[704,256]{1,0:T(8,128)(2,1)S(1)}, u32[]{:S(2)}, u32[]{:S(2)}) collective-permute-start(bf16[704,256]{1,0:T(8,128)(2,1)S(1)} %collective-permute-done.1.refs_2_), channel_id=1, source_target_pairs={{0,1},{1,0},{2,3},{3,2},{4,5},{5,4},{6,7},{7,6},{8,9},{9,8},{10,11... | collective-permute-start | bytes 1081352 | tf_op jit(solution)/shard_map/ppermute | solution.py:734
  24.4 13.6 %copy-start.18 = (bf16[704,256]{1,0:T(8,128)(2,1)}, bf16[704,256]{1,0:T(8,128)(2,1)S(1)}, u32[]{:S(2)}) copy-start(bf16[704,256]{1,0:T(8,128)(2,1)S(1)} %collective-permute-done.refs_1_) | copy-start | bytes 1081348
  26.7 40.6 %copy-start = (f32[3,1024]{1,0:T(4,128)S(1)}, f32[3,1024]{1,0:T(4,128)}, u32[]{:S(2)}) copy-start(f32[3,1024]{1,0:T(4,128)} %refs_9_.5) | copy-start | bytes 36868
  26.7 40.6 %copy-start.1 = (f32[3,768]{1,0:T(4,128)S(1)}, f32[3,768]{1,0:T(4,128)}, u32[]{:S(2)}) copy-start(f32[3,768]{1,0:T(4,128)} %refs_8_.5) | copy-start | bytes 27652
  26.7 40.6 %copy-start.5 = (s32[2,256]{1,0:T(2,128)S(1)}, s32[2,256]{1,0:T(2,128)}, u32[]{:S(2)}) copy-start(s32[2,256]{1,0:T(2,128)} %refs_8_.4) | copy-start | bytes 6148
  26.7 40.6 %copy-start.6 = (s32[2,160]{1,0:T(2,128)S(1)}, s32[2,160]{1,0:T(2,128)}, u32[]{:S(2)}) copy-start(s32[2,160]{1,0:T(2,128)} %refs_9_.4) | copy-start | bytes 3844
  33.2 53.7 %collective-permute-start.5 = (bf16[704,256]{1,0:T(8,128)(2,1)}, bf16[704,256]{1,0:T(8,128)(2,1)S(1)}, u32[]{:S(2)}, u32[]{:S(2)}) collective-permute-start(bf16[704,256]{1,0:T(8,128)(2,1)} %pack.3.refs_13_), channel_id=1, source_target_pairs={{0,3},{1,2},{2,1},{3,0},{4,7},{5,6},{6,5},{7,4},{8,11},{9,10},{10,... | collective-permute-start | bytes 1081352 | tf_op jit(solution)/shard_map/ppermute | solution.py:727
  37.4 49.5 %collective-permute-start.4 = (bf16[704,256]{1,0:T(8,128)(2,1)}, bf16[704,256]{1,0:T(8,128)(2,1)S(1)}, u32[]{:S(2)}, u32[]{:S(2)}) collective-permute-start(bf16[704,256]{1,0:T(8,128)(2,1)} %pack.3.refs_13_), channel_id=1, source_target_pairs={{0,2},{1,3},{2,0},{3,1},{4,6},{5,7},{6,4},{7,5},{8,10},{9,11},{10,... | collective-permute-start | bytes 1081352 | tf_op jit(solution)/shard_map/ppermute | solution.py:727
  37.4 49.5 %collective-permute-start.3 = (bf16[704,256]{1,0:T(8,128)(2,1)}, bf16[704,256]{1,0:T(8,128)(2,1)S(1)}, u32[]{:S(2)}, u32[]{:S(2)}) collective-permute-start(bf16[704,256]{1,0:T(8,128)(2,1)} %pack.3.refs_13_), channel_id=1, source_target_pairs={{0,1},{1,0},{2,3},{3,2},{4,5},{5,4},{6,7},{7,6},{8,9},{9,8},{10,11... | collective-permute-start | bytes 1081352 | tf_op jit(solution)/shard_map/ppermute | solution.py:727
  108.4 11.3 %collective-permute-start.6 = (bf16[4,768,256]{2,1,0:T(8,128)(2,1)}, bf16[4,768,256]{2,1,0:T(8,128)(2,1)S(1)}, u32[]{:S(2)}, u32[]{:S(2)}) collective-permute-start(bf16[4,768,256]{2,1,0:T(8,128)(2,1)} %get-tuple-element.173), channel_id=1, source_target_pairs={{0,4},{4,0},{8,12},{12,8},{16,20},{20,16},{24,28},{28,24},{1,5},{5... | collective-permute-start | bytes 4718600 | tf_op jit(solution)/shard_map/ppermute | solution.py:790
  121.3 24.0 %all-to-all-start = ((bf16[4,768,256]{2,1,0:T(8,128)(2,1)}), bf16[4,768,256]{2,1,0:T(8,128)(2,1)S(1)}, u32[]{:S(2)}, u32[]{:S(2)}) async-start(bf16[4,768,256]{2,1,0:T(8,128)(2,1)} %add_convert_fusion.2), calls=%async_computation | async-start | bytes 3145728 | tf_op jit(solution)/shard_map/all_to_all | solution.py:797
  145.3 8.5 %collective-permute-start.10 = (bf16[4,1056,256]{2,1,0:T(8,128)(2,1)}, bf16[4,1056,256]{2,1,0:T(8,128)(2,1)S(1)}, u32[]{:S(2)}, u32[]{:S(2)}) collective-permute-start(bf16[4,1056,256]{2,1,0:T(8,128)(2,1)} %get-tuple-element.203), channel_id=1, source_target_pairs={{0,4},{4,0},{8,12},{12,8},{16,20},{20,16},{24,28},{28,24},{1,5},{5... | collective-permute-start | bytes 6488072 | tf_op jit(solution)/shard_map/ppermute | solution.py:790
  155.8 31.3 %all-to-all-start.1 = ((bf16[4,1056,256]{2,1,0:T(8,128)(2,1)}), bf16[4,1056,256]{2,1,0:T(8,128)(2,1)S(1)}, u32[]{:S(2)}, u32[]{:S(2)}) async-start(bf16[4,1056,256]{2,1,0:T(8,128)(2,1)} %add_convert_fusion.1), calls=%async_computation.1 | async-start | bytes 4325376 | tf_op jit(solution)/shard_map/all_to_all | solution.py:797
  162.1 24.2 %collective-permute-start.9 = (bf16[768,256]{1,0:T(8,128)(2,1)}, bf16[768,256]{1,0:T(8,128)(2,1)S(1)}, u32[]{:S(2)}, u32[]{:S(2)}) collective-permute-start(bf16[768,256]{1,0:T(8,128)(2,1)} %reduce_sum.36.refs_0_), channel_id=1, source_target_pairs={{0,1},{1,0},{2,3},{3,2},{4,5},{5,4},{6,7},{7,6},{8,9},{9,8},{10,11... | collective-permute-start | bytes 1179656 | tf_op jit(solution)/shard_map/ppermute | solution.py:734
  163.6 23.5 %collective-permute-start.7 = (bf16[768,256]{1,0:T(8,128)(2,1)}, bf16[768,256]{1,0:T(8,128)(2,1)}, u32[]{:S(2)}, u32[]{:S(2)}) collective-permute-start(bf16[768,256]{1,0:T(8,128)(2,1)} %reduce_sum.36.refs_0_), channel_id=1, source_target_pairs={{0,2},{1,3},{2,0},{3,1},{4,6},{5,7},{6,4},{7,5},{8,10},{9,11},{10,... | collective-permute-start | bytes 1179656 | tf_op jit(solution)/shard_map/ppermute | solution.py:734
  187.1 12.6 %collective-permute-start.12 = (bf16[4,1184,256]{2,1,0:T(8,128)(2,1)}, bf16[4,1184,256]{2,1,0:T(8,128)(2,1)}, u32[]{:S(2)}, u32[]{:S(2)}) collective-permute-start(bf16[4,1184,256]{2,1,0:T(8,128)(2,1)} %get-tuple-element.238), channel_id=1, source_target_pairs={{0,4},{4,0},{8,12},{12,8},{16,20},{20,16},{24,28},{28,24},{1,5},{5... | collective-permute-start | bytes 7274504 | tf_op jit(solution)/shard_map/ppermute | solution.py:790
  187.1 11.8 %collective-permute-start.11 = (bf16[4,640,256]{2,1,0:T(8,128)(2,1)}, bf16[4,640,256]{2,1,0:T(8,128)(2,1)S(1)}, u32[]{:S(2)}, u32[]{:S(2)}) collective-permute-start(bf16[4,640,256]{2,1,0:T(8,128)(2,1)} %get-tuple-element.237), channel_id=1, source_target_pairs={{0,4},{4,0},{8,12},{12,8},{16,20},{20,16},{24,28},{28,24},{1,5},{5... | collective-permute-start | bytes 3932168 | tf_op jit(solution)/shard_map/ppermute | solution.py:790
  187.6 11.3 %collective-permute-start.8 = (bf16[768,256]{1,0:T(8,128)(2,1)}, bf16[768,256]{1,0:T(8,128)(2,1)S(1)}, u32[]{:S(2)}, u32[]{:S(2)}) collective-permute-start(bf16[768,256]{1,0:T(8,128)(2,1)} %collective-permute-done.7.refs_2_), channel_id=1, source_target_pairs={{0,1},{1,0},{2,3},{3,2},{4,5},{5,4},{6,7},{7,6},{8,9},{9,8},{10,11... | collective-permute-start | bytes 1179656 | tf_op jit(solution)/shard_map/ppermute | solution.py:734
  201.1 32.3 %all-to-all-start.2 = ((bf16[4,640,256]{2,1,0:T(8,128)(2,1)}), bf16[4,640,256]{2,1,0:T(8,128)(2,1)S(1)}, u32[]{:S(2)}, u32[]{:S(2)}) async-start(bf16[4,640,256]{2,1,0:T(8,128)(2,1)} %add_convert_fusion.3), calls=%async_computation.2 | async-start | bytes 2621440 | tf_op jit(solution)/shard_map/all_to_all | solution.py:797
  206.7 25.8 %collective-permute-start.14 = (bf16[1056,256]{1,0:T(8,128)(2,1)}, bf16[1056,256]{1,0:T(8,128)(2,1)S(1)}, u32[]{:S(2)}, u32[]{:S(2)}) collective-permute-start(bf16[1056,256]{1,0:T(8,128)(2,1)} %reduce_sum.37.refs_0_), channel_id=1, source_target_pairs={{0,2},{1,3},{2,0},{3,1},{4,6},{5,7},{6,4},{7,5},{8,10},{9,11},{10,... | collective-permute-start | bytes 1622024 | tf_op jit(solution)/shard_map/ppermute | solution.py:734
  207.2 26.2 %collective-permute-start.13 = (bf16[1056,256]{1,0:T(8,128)(2,1)}, bf16[1056,256]{1,0:T(8,128)(2,1)}, u32[]{:S(2)}, u32[]{:S(2)}) collective-permute-start(bf16[1056,256]{1,0:T(8,128)(2,1)} %reduce_sum.37.refs_0_), channel_id=1, source_target_pairs={{0,1},{1,0},{2,3},{3,2},{4,5},{5,4},{6,7},{7,6},{8,9},{9,8},{10,11... | collective-permute-start | bytes 1622024 | tf_op jit(solution)/shard_map/ppermute | solution.py:734
  234.4 33.4 %all-to-all-start.3 = ((bf16[4,1184,256]{2,1,0:T(8,128)(2,1)}), bf16[4,1184,256]{2,1,0:T(8,128)(2,1)S(1)}, u32[]{:S(2)}, u32[]{:S(2)}) async-start(bf16[4,1184,256]{2,1,0:T(8,128)(2,1)} %add_convert_fusion), calls=%async_computation.3 | async-start | bytes 4849664 | tf_op jit(solution)/shard_map/all_to_all | solution.py:797
  240.0 30.4 %copy-start.12 = (bf16[640,256]{1,0:T(8,128)(2,1)}, bf16[640,256]{1,0:T(8,128)(2,1)S(1)}, u32[]{:S(2)}) copy-start(bf16[640,256]{1,0:T(8,128)(2,1)S(1)} %reduce_sum.38.refs_0_) | copy-start | bytes 983044
  240.0 16.6 %collective-permute-start.16 = (bf16[640,256]{1,0:T(8,128)(2,1)S(1)}, bf16[640,256]{1,0:T(8,128)(2,1)S(1)}, u32[]{:S(2)}, u32[]{:S(2)}) collective-permute-start(bf16[640,256]{1,0:T(8,128)(2,1)S(1)} %reduce_sum.38.refs_0_), channel_id=1, source_target_pairs={{0,2},{1,3},{2,0},{3,1},{4,6},{5,7},{6,4},{7,5},{8,10},{9,11},{10,... | collective-permute-start | bytes 983048 | tf_op jit(solution)/shard_map/ppermute | solution.py:734
  240.1 22.6 %collective-permute-start.18 = (bf16[1056,256]{1,0:T(8,128)(2,1)}, bf16[1056,256]{1,0:T(8,128)(2,1)S(1)}, u32[]{:S(2)}, u32[]{:S(2)}) collective-permute-start(bf16[1056,256]{1,0:T(8,128)(2,1)} %copy-done.13), channel_id=1, source_target_pairs={{0,1},{1,0},{2,3},{3,2},{4,5},{5,4},{6,7},{7,6},{8,9},{9,8},{10,11... | collective-permute-start | bytes 1622024 | tf_op jit(solution)/shard_map/ppermute | solution.py:734
  242.4 28.0 %collective-permute-start.15 = (bf16[640,256]{1,0:T(8,128)(2,1)S(1)}, bf16[640,256]{1,0:T(8,128)(2,1)S(1)}, u32[]{:S(2)}, u32[]{:S(2)}) collective-permute-start(bf16[640,256]{1,0:T(8,128)(2,1)S(1)} %reduce_sum.38.refs_0_), channel_id=1, source_target_pairs={{0,1},{1,0},{2,3},{3,2},{4,5},{5,4},{6,7},{7,6},{8,9},{9,8},{10,11... | collective-permute-start | bytes 983048 | tf_op jit(solution)/shard_map/ppermute | solution.py:734
  256.6 13.8 %copy-start.23 = (bf16[640,256]{1,0:T(8,128)(2,1)}, bf16[640,256]{1,0:T(8,128)(2,1)S(1)}, u32[]{:S(2)}) copy-start(bf16[640,256]{1,0:T(8,128)(2,1)S(1)} %collective-permute-done.16.refs_2_) | copy-start | bytes 983044
  256.6 19.1 %collective-permute-start.17 = (bf16[640,256]{1,0:T(8,128)(2,1)S(1)}, bf16[640,256]{1,0:T(8,128)(2,1)}, u32[]{:S(2)}, u32[]{:S(2)}) collective-permute-start(bf16[640,256]{1,0:T(8,128)(2,1)S(1)} %collective-permute-done.16.refs_2_), channel_id=1, source_target_pairs={{0,1},{1,0},{2,3},{3,2},{4,5},{5,4},{6,7},{7,6},{8,9},{9,8},{10,11... | collective-permute-start | bytes 983048 | tf_op jit(solution)/shard_map/ppermute | solution.py:734
  (16 other events, 61.7 us)
where the time goes:
time: 284 us; the launch traced here: 280 us
  Pallas kernels  152 us (54%)
  waiting for transfers between devices  68.2 us (24%)
  starting transfers between devices  36.9 us (13%)
  other arithmetic  14.8 us (5%)
  local copies, waits for them, and re-layouts  5.78 us (2%)
    pallas_call x14, Pallas kernels, kernel_call(): pl.pallas_call(kernel, in_specs=[pl.BlockSpec(memory_space=pltpu.SMEM)] +...  152 us
    ppermute x12, waiting for transfers between devices, pieces(): lax.ppermute(got[k ^ step], 'seq', [(i, i ^ step) for i in range(n)])  65 us
    all_to_all x4, starting transfers between devices, cross(): lax.all_to_all(self.pair, 'dp', split_axis=0, concat_axis=0, tiled=True,...  16.1 us
    ppermute x12, starting transfers between devices, pieces(): lax.ppermute(got[k ^ step], 'seq', [(i, i ^ step) for i in range(n)])  15.4 us
    convert_element_type x4, other arithmetic, add(): self.pair = (self.keep.astype(F32) + self.got.astype(F32)).astype(BF16)  9.33 us
    unnamed x50, local copies, waits for them, and re-layouts  5.78 us
  transfers between devices with their start and end apart: 23, of which 8 were waited for; matrix products, arithmetic and copies ran while one was open for 3% of the time, Pallas kernels for 45%

commit v1 on v0

--- a/solution.py
+++ b/solution.py
@@ -517,7 +517,7 @@
 
 
 def qkv_back_body(scal, k, cp):
-    wa = chunked(cp, k.qkv_t, k.wa, 0, 2)
+    wa = chunked(cp, k.qkv_t, k.wa, 0, 3)
     extra_t = [cp.fetch(k.h_tn2, k.tn2), cp.fetch(k.h_tr2, k.tr2)]
     wb = chunked(cp, k.qkv_i, k.wb, 0, 2)
     extra_i = [cp.fetch(k.h_in2, k.in2), cp.fetch(k.h_ir2, k.ir2)]

time: 284 us -> 286 us (level)
  no operation moved by 1% of the time
where the time goes in v1:
time: 286 us; the launch traced here: 281 us
  Pallas kernels  154 us (54%)
  waiting for transfers between devices  68.2 us (24%)
  starting transfers between devices  36.9 us (13%)
  other arithmetic  14.8 us (5%)
  local copies, waits for them, and re-layouts  5.78 us (2%)
    pallas_call x14, Pallas kernels, kernel_call(): pl.pallas_call(kernel, in_specs=[pl.BlockSpec(memory_space=pltpu.SMEM)] +...  154 us
    ppermute x12, waiting for transfers between devices, pieces(): lax.ppermute(got[k ^ step], 'seq', [(i, i ^ step) for i in range(n)])  65 us
    all_to_all x4, starting transfers between devices, cross(): lax.all_to_all(self.pair, 'dp', split_axis=0, concat_axis=0, tiled=True,...  16.2 us
    ppermute x12, starting transfers between devices, pieces(): lax.ppermute(got[k ^ step], 'seq', [(i, i ^ step) for i in range(n)])  15.4 us
    convert_element_type x4, other arithmetic, add(): self.pair = (self.keep.astype(F32) + self.got.astype(F32)).astype(BF16)  9.33 us
    unnamed x50, local copies, waits for them, and re-layouts  5.78 us
  transfers between devices with their start and end apart: 23, of which 8 were waited for; matrix products, arithmetic and copies ran while one was open for 3% of the time, Pallas kernels for 45%

profile of v1, /device:TPU:0, one launch (start us, length us, event | category | flops | bytes accessed | tf_op | source)
XLA Modules:
  0.0 281.3 jit_solution(3317669695543803932)
XLA Ops:
  0.7 2.3 pack.2.refs_0_
  3.1 4.1 %collective-permute-start.1 = (bf16[704,256]{1,0:T(8,128)(2,1)}, bf16[704,256]{1,0:T(8,128)(2,1)S(1)}, u32[]{:S(2)}, u32[]{:S(2)}) collective-permute-start(bf16[704,256]{1,0:T(8,128)(2,1)} %pack.2.refs_0_), channel_id=1, source_target_pairs={{0,2},{1,3},{2,0},{3,1},{4,6},{5,7},{6,4},{7,5},{8,10},{9,11},{10,... | collective-permute-start | bytes 1081352 | tf_op jit(solution)/shard_map/ppermute | solution.py:734
  8.8 14.9 %collective-permute-done.1.refs_2_ = bf16[704,256]{1,0:T(8,128)(2,1)S(1)} collective-permute-done((bf16[704,256]{1,0:T(8,128)(2,1)}, bf16[704,256]{1,0:T(8,128)(2,1)S(1)}, u32[]{:S(2)}, u32[]{:S(2)}) %collective-permute-start.1) | collective-permute-done | bytes 360480 | tf_op jit(solution)/shard_map/ppermute | solution.py:734
  24.4 2.3 pack.3.refs_13_
  26.7 6.4 %collective-permute-done.2.refs_3_ = bf16[704,256]{1,0:T(8,128)(2,1)S(1)} collective-permute-done((bf16[704,256]{1,0:T(8,128)(2,1)S(1)}, bf16[704,256]{1,0:T(8,128)(2,1)S(1)}, u32[]{:S(2)}, u32[]{:S(2)}) %collective-permute-start.2) | collective-permute-done | bytes 360480 | tf_op jit(solution)/shard_map/ppermute | solution.py:734
  33.2 4.2 %collective-permute-start.5 = (bf16[704,256]{1,0:T(8,128)(2,1)}, bf16[704,256]{1,0:T(8,128)(2,1)S(1)}, u32[]{:S(2)}, u32[]{:S(2)}) collective-permute-start(bf16[704,256]{1,0:T(8,128)(2,1)} %pack.3.refs_13_), channel_id=1, source_target_pairs={{0,3},{1,2},{2,1},{3,0},{4,7},{5,6},{6,5},{7,4},{8,11},{9,10},{10,... | collective-permute-start | bytes 1081352 | tf_op jit(solution)/shard_map/ppermute | solution.py:727
  38.0 29.3 %co_stage.1 = (bf16[512,768]{1,0:T(8,128)(2,1)}, bf16[320,1024]{1,0:T(8,128)(2,1)}, bf16[512,3072]{1,0:T(8,128)(2,1)}, bf16[320,3072]{1,0:T(8,128)(2,1)}, bf16[5...) custom-call(s32[2]{0:T(128)} %copy-done.2, ...), custom_call_target="tpu_custom_call" | custom-call | tf_op jit(solution)/shard_map/co_stage/pallas_call | solution.py:91
  68.0 18.8 %self_stage.1 = (bf16[512,2304]{1,0:T(8,128)(2,1)}, bf16[320,3072]{1,0:T(8,128)(2,1)}, bf16[512,768]{1,0:T(8,128)(2,1)}, bf16[320,1024]{1,0:T(8,128)(2,1)}, bf16...) custom-call(s32[2]{0:T(128)S(1)} %copy-done.3, ...), custom_call_target="tpu_custom_call" | custom-call | tf_op jit(solution)/shard_map/self_stage/pallas_call | solution.py:91
  87.8 20.6 %self_back.1 = (bf16[4,768,256]{2,1,0:T(8,128)(2,1)}, bf16[4,768,256]{2,1,0:T(8,128)(2,1)}, bf16[320,1024]{1,0:T(8,128)(2,1)}, f32[512,768]{1,0:T(8,128)S(1)}, f...) custom-call(s32[2]{0:T(128)S(1)} %copy-done.3, ...), custom_call_target="tpu_custom_call" | custom-call | tf_op jit(solution)/shard_map/self_back/pallas_call | solution.py:91
  108.5 13.0 %qkv_back.1 = (f32[512,768]{1,0:T(8,128)}, f32[320,1024]{1,0:T(8,128)}, bf16[512,768]{1,0:T(8,128)(2,1)}, bf16[320,1024]{1,0:T(8,128)(2,1)}, f32[8,768]{1,0:T(8,128)}, /*index=5*/f32[8,1024]{1,0:T(8,128)}) custom-call(s32[2]{0:T(128)S(1)} %copy-done.3, f32[512,768]{1,0:T(8,128)} %get-tuple-element.158.refs_2_.refs_0_, ...), custom_call_target="tpu_custom_call" | custom-call | tf_op jit(solution)/shard_map/qkv_back/pallas_call | solution.py:91
  123.1 4.0 %all-to-all-start = ((bf16[4,768,256]{2,1,0:T(8,128)(2,1)}), bf16[4,768,256]{2,1,0:T(8,128)(2,1)S(1)}, u32[]{:S(2)}, u32[]{:S(2)}) async-start(bf16[4,768,256]{2,1,0:T(8,128)(2,1)} %add_convert_fusion.2), calls=%async_computation | async-start | bytes 3145728 | tf_op jit(solution)/shard_map/all_to_all | solution.py:797
  127.1 16.8 %ffn_back.1 = (bf16[4,1056,256]{2,1,0:T(8,128)(2,1)}, bf16[4,1056,256]{2,1,0:T(8,128)(2,1)}, f32[512,768]{1,0:T(8,128)}, f32[320,1024]{1,0:T(8,128)}) custom-call(s32[2]{0:T(128)S(1)} %copy-done.4, bf16[1024,1024]{1,0:T(8,128)(2,1)} %refs_0_.5, bf16[320,1024]{1,0:T(8,128)(2,1)} %get-tuple-element.185.refs_1_, bf16[1024,1024]{1,0:T(8,128)(2,1)} %refs_2_.3, ...), custom_call_target="tpu_custom_call" | custom-call | tf_op jit(solution)/shard_map/ffn_back/pallas_call | solution.py:91
  143.9 3.1 %all-to-all-done = bf16[4,768,256]{2,1,0:T(8,128)(2,1)S(1)} async-done(((bf16[4,768,256]{2,1,0:T(8,128)(2,1)}), bf16[4,768,256]{2,1,0:T(8,128)(2,1)S(1)}, u32[]{:S(2)}, u32[]{:S(2)}) %all-to-all-start) | async-done | bytes 1572896 | tf_op jit(solution)/shard_map/all_to_all | solution.py:797
  147.1 8.5 %first_norm_back.1 = (bf16[512,768]{1,0:T(8,128)(2,1)}, bf16[320,1024]{1,0:T(8,128)(2,1)}, bf16[512,1024]{1,0:T(8,128)(2,1)}, bf16[320,1024]{1,0:T(8,128)(2,1)},...) custom-call(s32[2]{0:T(128)S(1)} %copy-done.4, ...), custom_call_target="tpu_custom_call" | custom-call | tf_op jit(solution)/shard_map/first_norm_back/pallas_call | solution.py:91
  157.6 3.8 %all-to-all-start.1 = ((bf16[4,1056,256]{2,1,0:T(8,128)(2,1)}), bf16[4,1056,256]{2,1,0:T(8,128)(2,1)S(1)}, u32[]{:S(2)}, u32[]{:S(2)}) async-start(bf16[4,1056,256]{2,1,0:T(8,128)(2,1)} %add_convert_fusion.1), calls=%async_computation.1 | async-start | bytes 4325376 | tf_op jit(solution)/shard_map/all_to_all | solution.py:797
  161.4 2.5 reduce_sum.36.refs_0_
  165.3 2.9 %collective-permute-start.7 = (bf16[768,256]{1,0:T(8,128)(2,1)}, bf16[768,256]{1,0:T(8,128)(2,1)}, u32[]{:S(2)}, u32[]{:S(2)}) collective-permute-start(bf16[768,256]{1,0:T(8,128)(2,1)} %reduce_sum.36.refs_0_), channel_id=1, source_target_pairs={{0,2},{1,3},{2,0},{3,1},{4,6},{5,7},{6,4},{7,5},{8,10},{9,11},{10,... | collective-permute-start | bytes 1179656 | tf_op jit(solution)/shard_map/ppermute | solution.py:734
  168.3 19.8 %co_back.1 = (bf16[4,640,256]{2,1,0:T(8,128)(2,1)}, bf16[4,640,256]{2,1,0:T(8,128)(2,1)}, bf16[4,1184,256]{2,1,0:T(8,128)(2,1)}, bf16[4,1184,256]{2,1,0:T(8,128)...) custom-call(s32[2]{0:T(128)S(1)} %copy-done.4, bf16[512,3072]{1,0:T(8,128)(2,1)} %get-tuple-element.213.refs_0_, ...), custom_call_target="tpu_custom_call" | custom-call | tf_op jit(solution)/shard_map/co_back/pallas_call | solution.py:91
  189.4 8.7 %in_back.1 = (f32[2,64,768]{2,1,0:T(8,128)}, f32[2,40,1024]{2,1,0:T(8,128)}) custom-call(s32[2]{0:T(128)S(1)} %copy-done.4, bf16[768,3072]{1,0:T(8,128)(2,1)} %refs_0_.6, bf16[1024,3072]{1,0:T(8,128)(2,1)} %refs_1_.4, bf16[2,64,3072]{2,1,0:T(8,128)(2,1)S(1)} %get-tuple-element.239.refs_2_, bf16[2,40,3072]{2,1,0:T(8,128)(2,1)S(1)} %get-tuple-element.240.refs_3_, ...), custom_call_target="tpu_custom_call" | custom-call | tf_op jit(solution)/shard_map/in_back/pallas_call | solution.py:91
  198.1 2.6 collective-permute-done.8.refs_3_
  202.8 4.4 %all-to-all-start.2 = ((bf16[4,640,256]{2,1,0:T(8,128)(2,1)}), bf16[4,640,256]{2,1,0:T(8,128)(2,1)S(1)}, u32[]{:S(2)}, u32[]{:S(2)}) async-start(bf16[4,640,256]{2,1,0:T(8,128)(2,1)} %add_convert_fusion.3), calls=%async_computation.2 | async-start | bytes 2621440 | tf_op jit(solution)/shard_map/all_to_all | solution.py:797
  210.7 4.4 %add_convert_fusion = bf16[4,1184,256]{2,1,0:T(8,128)(2,1)} fusion(bf16[4,1184,256]{2,1,0:T(8,128)(2,1)} %collective-permute-done.12, bf16[4,1184,256]{2,1,0:T(8,128)(2,1)} %get-tuple-element.250), kind=kLoop, calls=%fused_computation | loop fusion | flops 4849664 | bytes 7274496 | tf_op jit(solution)/shard_map/convert_element_type | solution.py:793
  215.0 19.3 %collective-permute-done.14.refs_2_ = bf16[1056,256]{1,0:T(8,128)(2,1)S(1)} collective-permute-done((bf16[1056,256]{1,0:T(8,128)(2,1)}, bf16[1056,256]{1,0:T(8,128)(2,1)S(1)}, u32[]{:S(2)}, u32[]{:S(2)}) %collective-permute-start.14) | collective-permute-done | bytes 540704 | tf_op jit(solution)/shard_map/ppermute | solution.py:734
  236.2 3.9 %all-to-all-start.3 = ((bf16[4,1184,256]{2,1,0:T(8,128)(2,1)}), bf16[4,1184,256]{2,1,0:T(8,128)(2,1)S(1)}, u32[]{:S(2)}, u32[]{:S(2)}) async-start(bf16[4,1184,256]{2,1,0:T(8,128)(2,1)} %add_convert_fusion), calls=%async_computation.3 | async-start | bytes 4849664 | tf_op jit(solution)/shard_map/all_to_all | solution.py:797
  241.8 2.3 collective-permute-start.18
  244.2 14.2 %collective-permute-done.16.refs_2_ = bf16[640,256]{1,0:T(8,128)(2,1)S(1)} collective-permute-done((bf16[640,256]{1,0:T(8,128)(2,1)S(1)}, bf16[640,256]{1,0:T(8,128)(2,1)S(1)}, u32[]{:S(2)}, u32[]{:S(2)}) %collective-permute-start.16) | collective-permute-done | bytes 327712 | tf_op jit(solution)/shard_map/ppermute | solution.py:734
  258.4 3.7 %unpack.7 = (f32[96,768]{1,0:T(8,128)}, f32[96,2304]{1,0:T(8,128)}, f32[128,3072]{1,0:T(8,128)}) custom-call(s32[2]{0:T(128)S(1)} %copy-done.4, bf16[768,256]{1,0:T(8,128)(2,1)} %reduce_sum.36.refs_0_, bf16[768,256]{1,0:T(8,128)(2,1)} %copy-done.15, bf16[768,256]{1,0:T(8,128)(2,1)} %collective-permute-done.7.refs_2_, bf16[768,256]{1,0:T(8,128)(2,1)} %copy-done.16), custom_call_target="tpu_custom_call" | custom-call | tf_op jit(solution)/shard_map/unpack/pallas_call | solution.py:91
  262.1 2.4 collective-permute-done.18.refs_3_
  265.2 4.3 %unpack.6 = (f32[384,768]{1,0:T(8,128)}, f32[128,1024]{1,0:T(8,128)}, f32[96,3072]{1,0:T(8,128)}, f32[128,1024]{1,0:T(8,128)}, f32[128,1024]{1,0:T(8,128)}) custom-call(s32[2]{0:T(128)S(1)} %copy-done.4, bf16[1056,256]{1,0:T(8,128)(2,1)} %reduce_sum.37.refs_0_, bf16[1056,256]{1,0:T(8,128)(2,1)} %collective-permute-done.13.refs_1_, ...), custom_call_target="tpu_custom_call" | custom-call | tf_op jit(solution)/shard_map/unpack/pallas_call | solution.py:91
  269.6 2.6 unpack.4
  272.2 5.3 %collective-permute-done.17.refs_3_ = bf16[640,256]{1,0:T(8,128)(2,1)} collective-permute-done((bf16[640,256]{1,0:T(8,128)(2,1)S(1)}, bf16[640,256]{1,0:T(8,128)(2,1)}, u32[]{:S(2)}, u32[]{:S(2)}) %collective-permute-start.17) | collective-permute-done | bytes 327712 | tf_op jit(solution)/shard_map/ppermute | solution.py:734
  277.4 3.5 %unpack.5 = (f32[128,1024]{1,0:T(8,128)}, f32[128,3072]{1,0:T(8,128)}, f32[128,768]{1,0:T(8,128)}) custom-call(s32[2]{0:T(128)S(1)} %copy-done.4, bf16[640,256]{1,0:T(8,128)(2,1)} %copy-done.12, bf16[640,256]{1,0:T(8,128)(2,1)} %copy-done.24, bf16[640,256]{1,0:T(8,128)(2,1)} %copy-done.23, bf16[640,256]{1,0:T(8,128)(2,1)} %collective-permute-done.17.refs_3_), custom_call_target="tpu_custom_call" | custom-call | tf_op jit(solution)/shard_map/unpack/pallas_call | solution.py:91
  (86 shorter events, 20.9 us)
Async XLA Ops:
  0.7 37.2 %copy-start.2 = (s32[2]{0:T(128)}, s32[2]{0:T(128)S(1)}, u32[]{:S(2)}) copy-start(s32[2]{0:T(128)S(1)} %pad_add_fusion.scal_ref) | copy-start | bytes 28
  3.1 20.6 %collective-permute-start.1 = (bf16[704,256]{1,0:T(8,128)(2,1)}, bf16[704,256]{1,0:T(8,128)(2,1)S(1)}, u32[]{:S(2)}, u32[]{:S(2)}) collective-permute-start(bf16[704,256]{1,0:T(8,128)(2,1)} %pack.2.refs_0_), channel_id=1, source_target_pairs={{0,2},{1,3},{2,0},{3,1},{4,6},{5,7},{6,4},{7,5},{8,10},{9,11},{10,... | collective-permute-start | bytes 1081352 | tf_op jit(solution)/shard_map/ppermute | solution.py:734
  7.2 17.2 %collective-permute-start = (bf16[704,256]{1,0:T(8,128)(2,1)}, bf16[704,256]{1,0:T(8,128)(2,1)S(1)}, u32[]{:S(2)}, u32[]{:S(2)}) collective-permute-start(bf16[704,256]{1,0:T(8,128)(2,1)} %pack.2.refs_0_), channel_id=1, source_target_pairs={{0,1},{1,0},{2,3},{3,2},{4,5},{5,4},{6,7},{7,6},{8,9},{9,8},{10,11... | collective-permute-start | bytes 1081352 | tf_op jit(solution)/shard_map/ppermute | solution.py:734
  23.6 14.3 %copy-start.17 = (bf16[704,256]{1,0:T(8,128)(2,1)}, bf16[704,256]{1,0:T(8,128)(2,1)S(1)}, u32[]{:S(2)}) copy-start(bf16[704,256]{1,0:T(8,128)(2,1)S(1)} %collective-permute-done.1.refs_2_) | copy-start | bytes 1081348
  23.6 9.5 %collective-permute-start.2 = (bf16[704,256]{1,0:T(8,128)(2,1)S(1)}, bf16[704,256]{1,0:T(8,128)(2,1)S(1)}, u32[]{:S(2)}, u32[]{:S(2)}) collective-permute-start(bf16[704,256]{1,0:T(8,128)(2,1)S(1)} %collective-permute-done.1.refs_2_), channel_id=1, source_target_pairs={{0,1},{1,0},{2,3},{3,2},{4,5},{5,4},{6,7},{7,6},{8,9},{9,8},{10,11... | collective-permute-start | bytes 1081352 | tf_op jit(solution)/shard_map/ppermute | solution.py:734
  24.4 13.6 %copy-start.18 = (bf16[704,256]{1,0:T(8,128)(2,1)}, bf16[704,256]{1,0:T(8,128)(2,1)S(1)}, u32[]{:S(2)}) copy-start(bf16[704,256]{1,0:T(8,128)(2,1)S(1)} %collective-permute-done.refs_1_) | copy-start | bytes 1081348
  26.7 40.6 %copy-start = (f32[3,1024]{1,0:T(4,128)S(1)}, f32[3,1024]{1,0:T(4,128)}, u32[]{:S(2)}) copy-start(f32[3,1024]{1,0:T(4,128)} %refs_9_.5) | copy-start | bytes 36868
  26.7 40.6 %copy-start.1 = (f32[3,768]{1,0:T(4,128)S(1)}, f32[3,768]{1,0:T(4,128)}, u32[]{:S(2)}) copy-start(f32[3,768]{1,0:T(4,128)} %refs_8_.5) | copy-start | bytes 27652
  26.7 40.6 %copy-start.5 = (s32[2,256]{1,0:T(2,128)S(1)}, s32[2,256]{1,0:T(2,128)}, u32[]{:S(2)}) copy-start(s32[2,256]{1,0:T(2,128)} %refs_8_.4) | copy-start | bytes 6148
  26.7 40.6 %copy-start.6 = (s32[2,160]{1,0:T(2,128)S(1)}, s32[2,160]{1,0:T(2,128)}, u32[]{:S(2)}) copy-start(s32[2,160]{1,0:T(2,128)} %refs_9_.4) | copy-start | bytes 3844
  33.2 53.7 %collective-permute-start.5 = (bf16[704,256]{1,0:T(8,128)(2,1)}, bf16[704,256]{1,0:T(8,128)(2,1)S(1)}, u32[]{:S(2)}, u32[]{:S(2)}) collective-permute-start(bf16[704,256]{1,0:T(8,128)(2,1)} %pack.3.refs_13_), channel_id=1, source_target_pairs={{0,3},{1,2},{2,1},{3,0},{4,7},{5,6},{6,5},{7,4},{8,11},{9,10},{10,... | collective-permute-start | bytes 1081352 | tf_op jit(solution)/shard_map/ppermute | solution.py:727
  37.4 49.5 %collective-permute-start.4 = (bf16[704,256]{1,0:T(8,128)(2,1)}, bf16[704,256]{1,0:T(8,128)(2,1)S(1)}, u32[]{:S(2)}, u32[]{:S(2)}) collective-permute-start(bf16[704,256]{1,0:T(8,128)(2,1)} %pack.3.refs_13_), channel_id=1, source_target_pairs={{0,2},{1,3},{2,0},{3,1},{4,6},{5,7},{6,4},{7,5},{8,10},{9,11},{10,... | collective-permute-start | bytes 1081352 | tf_op jit(solution)/shard_map/ppermute | solution.py:727
  37.4 49.5 %collective-permute-start.3 = (bf16[704,256]{1,0:T(8,128)(2,1)}, bf16[704,256]{1,0:T(8,128)(2,1)S(1)}, u32[]{:S(2)}, u32[]{:S(2)}) collective-permute-start(bf16[704,256]{1,0:T(8,128)(2,1)} %pack.3.refs_13_), channel_id=1, source_target_pairs={{0,1},{1,0},{2,3},{3,2},{4,5},{5,4},{6,7},{7,6},{8,9},{9,8},{10,11... | collective-permute-start | bytes 1081352 | tf_op jit(solution)/shard_map/ppermute | solution.py:727
  108.4 13.1 %collective-permute-start.6 = (bf16[4,768,256]{2,1,0:T(8,128)(2,1)}, bf16[4,768,256]{2,1,0:T(8,128)(2,1)S(1)}, u32[]{:S(2)}, u32[]{:S(2)}) collective-permute-start(bf16[4,768,256]{2,1,0:T(8,128)(2,1)} %get-tuple-element.173), channel_id=1, source_target_pairs={{0,4},{4,0},{8,12},{12,8},{16,20},{20,16},{24,28},{28,24},{1,5},{5... | collective-permute-start | bytes 4718600 | tf_op jit(solution)/shard_map/ppermute | solution.py:790
  123.1 24.0 %all-to-all-start = ((bf16[4,768,256]{2,1,0:T(8,128)(2,1)}), bf16[4,768,256]{2,1,0:T(8,128)(2,1)S(1)}, u32[]{:S(2)}, u32[]{:S(2)}) async-start(bf16[4,768,256]{2,1,0:T(8,128)(2,1)} %add_convert_fusion.2), calls=%async_computation | async-start | bytes 3145728 | tf_op jit(solution)/shard_map/all_to_all | solution.py:797
  147.1 8.5 %collective-permute-start.10 = (bf16[4,1056,256]{2,1,0:T(8,128)(2,1)}, bf16[4,1056,256]{2,1,0:T(8,128)(2,1)S(1)}, u32[]{:S(2)}, u32[]{:S(2)}) collective-permute-start(bf16[4,1056,256]{2,1,0:T(8,128)(2,1)} %get-tuple-element.203), channel_id=1, source_target_pairs={{0,4},{4,0},{8,12},{12,8},{16,20},{20,16},{24,28},{28,24},{1,5},{5... | collective-permute-start | bytes 6488072 | tf_op jit(solution)/shard_map/ppermute | solution.py:790
  157.6 31.3 %all-to-all-start.1 = ((bf16[4,1056,256]{2,1,0:T(8,128)(2,1)}), bf16[4,1056,256]{2,1,0:T(8,128)(2,1)S(1)}, u32[]{:S(2)}, u32[]{:S(2)}) async-start(bf16[4,1056,256]{2,1,0:T(8,128)(2,1)} %add_convert_fusion.1), calls=%async_computation.1 | async-start | bytes 4325376 | tf_op jit(solution)/shard_map/all_to_all | solution.py:797
  163.9 24.2 %collective-permute-start.9 = (bf16[768,256]{1,0:T(8,128)(2,1)}, bf16[768,256]{1,0:T(8,128)(2,1)S(1)}, u32[]{:S(2)}, u32[]{:S(2)}) collective-permute-start(bf16[768,256]{1,0:T(8,128)(2,1)} %reduce_sum.36.refs_0_), channel_id=1, source_target_pairs={{0,1},{1,0},{2,3},{3,2},{4,5},{5,4},{6,7},{7,6},{8,9},{9,8},{10,11... | collective-permute-start | bytes 1179656 | tf_op jit(solution)/shard_map/ppermute | solution.py:734
  165.3 23.5 %collective-permute-start.7 = (bf16[768,256]{1,0:T(8,128)(2,1)}, bf16[768,256]{1,0:T(8,128)(2,1)}, u32[]{:S(2)}, u32[]{:S(2)}) collective-permute-start(bf16[768,256]{1,0:T(8,128)(2,1)} %reduce_sum.36.refs_0_), channel_id=1, source_target_pairs={{0,2},{1,3},{2,0},{3,1},{4,6},{5,7},{6,4},{7,5},{8,10},{9,11},{10,... | collective-permute-start | bytes 1179656 | tf_op jit(solution)/shard_map/ppermute | solution.py:734
  188.9 12.6 %collective-permute-start.12 = (bf16[4,1184,256]{2,1,0:T(8,128)(2,1)}, bf16[4,1184,256]{2,1,0:T(8,128)(2,1)}, u32[]{:S(2)}, u32[]{:S(2)}) collective-permute-start(bf16[4,1184,256]{2,1,0:T(8,128)(2,1)} %get-tuple-element.238), channel_id=1, source_target_pairs={{0,4},{4,0},{8,12},{12,8},{16,20},{20,16},{24,28},{28,24},{1,5},{5... | collective-permute-start | bytes 7274504 | tf_op jit(solution)/shard_map/ppermute | solution.py:790
  188.9 11.8 %collective-permute-start.11 = (bf16[4,640,256]{2,1,0:T(8,128)(2,1)}, bf16[4,640,256]{2,1,0:T(8,128)(2,1)S(1)}, u32[]{:S(2)}, u32[]{:S(2)}) collective-permute-start(bf16[4,640,256]{2,1,0:T(8,128)(2,1)} %get-tuple-element.237), channel_id=1, source_target_pairs={{0,4},{4,0},{8,12},{12,8},{16,20},{20,16},{24,28},{28,24},{1,5},{5... | collective-permute-start | bytes 3932168 | tf_op jit(solution)/shard_map/ppermute | solution.py:790
  189.4 11.3 %collective-permute-start.8 = (bf16[768,256]{1,0:T(8,128)(2,1)}, bf16[768,256]{1,0:T(8,128)(2,1)S(1)}, u32[]{:S(2)}, u32[]{:S(2)}) collective-permute-start(bf16[768,256]{1,0:T(8,128)(2,1)} %collective-permute-done.7.refs_2_), channel_id=1, source_target_pairs={{0,1},{1,0},{2,3},{3,2},{4,5},{5,4},{6,7},{7,6},{8,9},{9,8},{10,11... | collective-permute-start | bytes 1179656 | tf_op jit(solution)/shard_map/ppermute | solution.py:734
  202.8 32.3 %all-to-all-start.2 = ((bf16[4,640,256]{2,1,0:T(8,128)(2,1)}), bf16[4,640,256]{2,1,0:T(8,128)(2,1)S(1)}, u32[]{:S(2)}, u32[]{:S(2)}) async-start(bf16[4,640,256]{2,1,0:T(8,128)(2,1)} %add_convert_fusion.3), calls=%async_computation.2 | async-start | bytes 2621440 | tf_op jit(solution)/shard_map/all_to_all | solution.py:797
  208.5 25.8 %collective-permute-start.14 = (bf16[1056,256]{1,0:T(8,128)(2,1)}, bf16[1056,256]{1,0:T(8,128)(2,1)S(1)}, u32[]{:S(2)}, u32[]{:S(2)}) collective-permute-start(bf16[1056,256]{1,0:T(8,128)(2,1)} %reduce_sum.37.refs_0_), channel_id=1, source_target_pairs={{0,2},{1,3},{2,0},{3,1},{4,6},{5,7},{6,4},{7,5},{8,10},{9,11},{10,... | collective-permute-start | bytes 1622024 | tf_op jit(solution)/shard_map/ppermute | solution.py:734
  208.9 26.2 %collective-permute-start.13 = (bf16[1056,256]{1,0:T(8,128)(2,1)}, bf16[1056,256]{1,0:T(8,128)(2,1)}, u32[]{:S(2)}, u32[]{:S(2)}) collective-permute-start(bf16[1056,256]{1,0:T(8,128)(2,1)} %reduce_sum.37.refs_0_), channel_id=1, source_target_pairs={{0,1},{1,0},{2,3},{3,2},{4,5},{5,4},{6,7},{7,6},{8,9},{9,8},{10,11... | collective-permute-start | bytes 1622024 | tf_op jit(solution)/shard_map/ppermute | solution.py:734
  236.2 33.4 %all-to-all-start.3 = ((bf16[4,1184,256]{2,1,0:T(8,128)(2,1)}), bf16[4,1184,256]{2,1,0:T(8,128)(2,1)S(1)}, u32[]{:S(2)}, u32[]{:S(2)}) async-start(bf16[4,1184,256]{2,1,0:T(8,128)(2,1)} %add_convert_fusion), calls=%async_computation.3 | async-start | bytes 4849664 | tf_op jit(solution)/shard_map/all_to_all | solution.py:797
  241.8 30.4 %copy-start.12 = (bf16[640,256]{1,0:T(8,128)(2,1)}, bf16[640,256]{1,0:T(8,128)(2,1)S(1)}, u32[]{:S(2)}) copy-start(bf16[640,256]{1,0:T(8,128)(2,1)S(1)} %reduce_sum.38.refs_0_) | copy-start | bytes 983044
  241.8 16.6 %collective-permute-start.16 = (bf16[640,256]{1,0:T(8,128)(2,1)S(1)}, bf16[640,256]{1,0:T(8,128)(2,1)S(1)}, u32[]{:S(2)}, u32[]{:S(2)}) collective-permute-start(bf16[640,256]{1,0:T(8,128)(2,1)S(1)} %reduce_sum.38.refs_0_), channel_id=1, source_target_pairs={{0,2},{1,3},{2,0},{3,1},{4,6},{5,7},{6,4},{7,5},{8,10},{9,11},{10,... | collective-permute-start | bytes 983048 | tf_op jit(solution)/shard_map/ppermute | solution.py:734
  241.8 22.6 %collective-permute-start.18 = (bf16[1056,256]{1,0:T(8,128)(2,1)}, bf16[1056,256]{1,0:T(8,128)(2,1)S(1)}, u32[]{:S(2)}, u32[]{:S(2)}) collective-permute-start(bf16[1056,256]{1,0:T(8,128)(2,1)} %copy-done.13), channel_id=1, source_target_pairs={{0,1},{1,0},{2,3},{3,2},{4,5},{5,4},{6,7},{7,6},{8,9},{9,8},{10,11... | collective-permute-start | bytes 1622024 | tf_op jit(solution)/shard_map/ppermute | solution.py:734
  244.2 28.0 %collective-permute-start.15 = (bf16[640,256]{1,0:T(8,128)(2,1)S(1)}, bf16[640,256]{1,0:T(8,128)(2,1)S(1)}, u32[]{:S(2)}, u32[]{:S(2)}) collective-permute-start(bf16[640,256]{1,0:T(8,128)(2,1)S(1)} %reduce_sum.38.refs_0_), channel_id=1, source_target_pairs={{0,1},{1,0},{2,3},{3,2},{4,5},{5,4},{6,7},{7,6},{8,9},{9,8},{10,11... | collective-permute-start | bytes 983048 | tf_op jit(solution)/shard_map/ppermute | solution.py:734
  258.3 13.8 %copy-start.23 = (bf16[640,256]{1,0:T(8,128)(2,1)}, bf16[640,256]{1,0:T(8,128)(2,1)S(1)}, u32[]{:S(2)}) copy-start(bf16[640,256]{1,0:T(8,128)(2,1)S(1)} %collective-permute-done.16.refs_2_) | copy-start | bytes 983044
  258.3 19.1 %collective-permute-start.17 = (bf16[640,256]{1,0:T(8,128)(2,1)S(1)}, bf16[640,256]{1,0:T(8,128)(2,1)}, u32[]{:S(2)}, u32[]{:S(2)}) collective-permute-start(bf16[640,256]{1,0:T(8,128)(2,1)S(1)} %collective-permute-done.16.refs_2_), channel_id=1, source_target_pairs={{0,1},{1,0},{2,3},{3,2},{4,5},{5,4},{6,7},{7,6},{8,9},{9,8},{10,11... | collective-permute-start | bytes 983048 | tf_op jit(solution)/shard_map/ppermute | solution.py:734
  (16 other events, 63.4 us)
